TPU v7x, 32 devices: a whole 2x2x4 slice. The times are simulated.
32 devices in a mesh: samp: 16 (over z, x, core), var: 2 (over y).
Axes of the slice: x: 2, y: 2, z: 4, core: 2. Of those that a mesh axis runs over, the one named last changes fastest.
Arguments:
- genotypes: bfloat16 [16384, 12288], P('samp', 'var'), may hold values from 0 to 2, as said below
- start_q: float32 [64, 16384], P(None, 'samp'), may hold values from 0 to 1, as said below
Outputs:
- final_q: float32 [64, 16384], P(None, 'samp')
- final_p: float32 [64, 12288], P(None, 'var')
Inputs may be any that keep to these rules, and one draw needn't show every extreme that they name: `genotypes`: genotype counts, whole numbers. `start_q`: nonnegative proportions.
All inputs are finite; a program needn't handle non-finite values.
Results may differ from a plain program's by a relative error of at most 0.001.
Values sent between devices are 32-bit elements; how exact they have to be, the bound alone decides.
No kernel may reach another device: no remote copies, remote signals or barrier semaphores. Data moves between devices by JAX's collectives and lax.ppermute only.
A program may use at most 64 MiB of HBM per device.

v0:
```python
import jax
import jax.numpy as jnp
from jax import lax
from jax.sharding import PartitionSpec as P

ITERS = 2


ridge_term = 1.0


def gram_solve(gram_matrix, right_side):
    eye_matrix = jnp.eye(gram_matrix.shape[0], dtype=jnp.float32)
    factor_low = jnp.linalg.cholesky(gram_matrix + ridge_term * eye_matrix)
    return jax.scipy.linalg.cho_solve((factor_low, True), right_side)


def body(genotypes, start_q):
    halved = genotypes * jnp.asarray(0.5, dtype=genotypes.dtype)
    ancestry = start_q
    frequency = None
    for iteration in range(ITERS):
        ancestry_b = ancestry.astype(jnp.bfloat16)
        cross_part = jnp.dot(ancestry_b, halved, preferred_element_type=jnp.float32)
        gram_part = jnp.dot(ancestry, ancestry.T, precision=lax.Precision.HIGHEST)
        width = cross_part.shape[1]
        summed = lax.psum(jnp.concatenate([cross_part, gram_part], axis=1), "samp")
        frequency = gram_solve(summed[:, width:], summed[:, :width])
        freq_b = frequency.astype(jnp.bfloat16)
        sample_part = lax.dot_general(
            freq_b, halved, (((1,), (1,)), ((), ())), preferred_element_type=jnp.float32
        )
        pgram_part = jnp.dot(frequency, frequency.T, precision=lax.Precision.HIGHEST)
        sample_share = lax.psum_scatter(sample_part, "var", scatter_dimension=1, tiled=True)
        gram_p = lax.psum(pgram_part, "var")
        ancestry_share = gram_solve(gram_p, sample_share)
        ancestry = lax.all_gather(ancestry_share, "var", axis=1, tiled=True)
    return (ancestry, frequency)


def solution(mesh):
    return jax.shard_map(
        body,
        mesh=mesh,
        in_specs=(P("samp", "var"), P(None, "samp")),
        out_specs=(P(None, "samp"), P(None, "var")),
        check_vma=False,
    )
```

profile of v0, /device:TPU:0, one launch (start us, length us, event | category | flops | bytes accessed | tf_op | source)
XLA Modules:
  0.0 362.6 jit_solution(11005803779710166309)
XLA Ops:
  7.2 1.4 fusion.55
  8.7 6.6 %fusion.8 = f32[64,6144]{0,1:T(8,128)S(1)} fusion(bf16[1024,6144]{1,0:T(8,128)(2,1)} %param.7, f32[64,1024]{1,0:T(8,128)} %param.8), kind=kOutput, calls=%fused_computation.8 | convolution fusion | flops 811663360 | bytes 14417920 | tf_op jit(solution)/shard_map/dot_general | solution.py:24
  15.3 1.9 pad_maximum_fusion
  17.2 0.2 reduce-scatter.3.cloned.1.call-start
  17.4 106.9 %all-reduce.3.cloned.1.call-done = f32[64,6208]{0,1:T(8,128)} async-done(((f32[64,6208]{0,1:T(8,128)}), f32[64,6208]{0,1:T(8,128)}) %all-reduce.3.cloned.1.call-update) | async-done | bytes 1589264 | tf_op jit(solution)/shard_map/psum | solution.py:27
  124.3 0.8 convert_add_fusion.3
  125.1 0.1 copy.6
  125.1 0.8 fusion.44
  125.9 5.8 %cholesky.74 = f32[64,64]{1,0:T(8,128)S(1)} custom-call(f32[64,64]{1,0:T(8,128)S(1)} %fusion.44), custom_call_target="Cholesky" | custom-call | tf_op jit(solution)/shard_map/jit(cholesky)/cholesky | solution.py:14
  131.8 0.6 compare_reduce_fusion.3
  132.4 0.7 fusion.23
  133.1 4.9 %custom-call.14 = f32[1,64,64]{1,2,0:T(8,128)S(1)} custom-call(f32[1,64,64]{2,1,0:T(8,128)S(1)} %fusion.23), custom_call_target="InvertDiagBlocksLowerTriangular" | custom-call | tf_op jit(solution)/shard_map/jit(_cho_solve)/triangular_solve | solution.py:15
  138.0 5.3 %fusion.17 = f32[64,6144]{1,0:T(8,128)S(1)} fusion(f32[64,6208]{0,1:T(8,128)} %all-reduce.3.cloned.1.call-done, f32[1,64,64]{1,2,0:T(8,128)S(1)} %custom-call.14), kind=kOutput, calls=%fused_computation.17 | convolution fusion | flops 301989888 | bytes 4734976 | tf_op jit(solution)/shard_map/jit(_cho_solve)/triangular_solve | solution.py:15
  143.3 1.5 fusion.41
  144.8 1.4 fusion.56
  146.2 9.2 %fusion.4 = f32[64,1024]{1,0:T(8,128)} fusion(bf16[1024,6144]{1,0:T(8,128)(2,1)} %param.7, f32[64,6144]{1,0:T(8,128)S(1)} %fusion.41), kind=kOutput, calls=%fused_computation.4 | convolution fusion | flops 811991040 | bytes 14417920 | tf_op jit(solution)/shard_map/dot_general | solution.py:30
  155.4 8.3 %psum.29 = f32[64,64]{0,1:T(8,128)S(1)} all-reduce(f32[64,64]{0,1:T(8,128)S(1)} %fusion.56), channel_id=1, replica_groups=mesh['samp'=16,'var'=2] {'var'}, use_global_device_ids=true, to_apply=%region_3.6 | all-reduce | flops 4096 | bytes 32768 | tf_op jit(solution)/shard_map/psum | solution.py:35
  163.7 0.3 all-reduce.5.cloned.1.call-start
  164.1 5.8 %cholesky.85 = f32[64,64]{1,0:T(8,128)S(1)} custom-call(f32[64,64]{1,0:T(8,128)S(1)} %fusion.40), custom_call_target="Cholesky" | custom-call | tf_op jit(solution)/shard_map/jit(cholesky)/cholesky | solution.py:14
  170.0 0.6 compare_reduce_fusion.2
  170.7 0.7 fusion.24
  171.3 4.9 %custom-call.15 = f32[1,64,64]{1,2,0:T(8,128)S(1)} custom-call(f32[1,64,64]{2,1,0:T(8,128)S(1)} %fusion.24), custom_call_target="InvertDiagBlocksLowerTriangular" | custom-call | tf_op jit(solution)/shard_map/jit(_cho_solve)/triangular_solve | solution.py:15
  176.2 1.2 fusion.38
  177.5 0.3 fusion.36
  177.7 5.6 %all_gather.6 = f32[64,1024]{1,0:T(8,128)S(1)} all-gather(f32[64,512]{1,0:T(8,128)S(1)} %fusion.36), channel_id=1, replica_groups=mesh['samp'=16,'var'=2] {'var'}, dimensions={1}, use_global_device_ids=true | all-gather | bytes 393216 | tf_op jit(solution)/shard_map/all_gather | solution.py:37
  183.4 0.4 fusion.57
  183.8 8.0 %fusion.2 = f32[64,6144]{0,1:T(8,128)S(1)} fusion(bf16[1024,6144]{1,0:T(8,128)(2,1)} %param.7, f32[64,1024]{1,0:T(8,128)S(1)} %all_gather.6), kind=kOutput, calls=%fused_computation.2 | convolution fusion | flops 811663360 | bytes 14417920 | tf_op jit(solution)/shard_map/dot_general | solution.py:24
  191.7 1.9 pad_maximum_fusion.1
  193.7 103.0 %all-reduce.5.cloned.1.call-done = f32[64,6208]{0,1:T(8,128)} async-done(((f32[64,6208]{0,1:T(8,128)}), f32[64,6208]{0,1:T(8,128)}) %all-reduce.5.cloned.1.call-update) | async-done | bytes 1589264 | tf_op jit(solution)/shard_map/psum | solution.py:27
  296.6 0.8 convert_add_fusion.1
  297.5 0.8 fusion.35
  298.3 5.8 %cholesky.96 = f32[64,64]{1,0:T(8,128)S(1)} custom-call(f32[64,64]{1,0:T(8,128)S(1)} %fusion.35), custom_call_target="Cholesky" | custom-call | tf_op jit(solution)/shard_map/jit(cholesky)/cholesky | solution.py:14
  304.1 0.6 compare_reduce_fusion.1
  304.8 0.7 fusion.25
  305.4 4.9 %custom-call.16 = f32[1,64,64]{1,2,0:T(8,128)S(1)} custom-call(f32[1,64,64]{2,1,0:T(8,128)S(1)} %fusion.25), custom_call_target="InvertDiagBlocksLowerTriangular" | custom-call | tf_op jit(solution)/shard_map/jit(_cho_solve)/triangular_solve | solution.py:15
  310.3 5.3 %fusion.15 = f32[64,6144]{1,0:T(8,128)S(1)} fusion(f32[64,6208]{0,1:T(8,128)} %all-reduce.5.cloned.1.call-done, f32[1,64,64]{1,2,0:T(8,128)S(1)} %custom-call.16), kind=kOutput, calls=%fused_computation.15 | convolution fusion | flops 301989888 | bytes 4734976 | tf_op jit(solution)/shard_map/jit(_cho_solve)/triangular_solve | solution.py:15
  315.7 1.5 fusion.32
  317.2 1.4 fusion.58
  318.6 9.2 %fusion = f32[64,1024]{1,0:T(8,128)} fusion(bf16[1024,6144]{1,0:T(8,128)(2,1)} %param.7, f32[64,6144]{1,0:T(8,128)S(1)} %fusion.32), kind=kOutput, calls=%fused_computation | convolution fusion | flops 811991040 | bytes 14417920 | tf_op jit(solution)/shard_map/dot_general | solution.py:30
  327.8 8.3 %psum.31 = f32[64,64]{0,1:T(8,128)S(1)} all-reduce(f32[64,64]{0,1:T(8,128)S(1)} %fusion.58), channel_id=1, replica_groups=mesh['samp'=16,'var'=2] {'var'}, use_global_device_ids=true, to_apply=%region_6.10 | all-reduce | flops 4096 | bytes 32768 | tf_op jit(solution)/shard_map/psum | solution.py:35
  336.2 5.8 %cholesky.107 = f32[64,64]{1,0:T(8,128)S(1)} custom-call(f32[64,64]{1,0:T(8,128)S(1)} %fusion.31), custom_call_target="Cholesky" | custom-call | tf_op jit(solution)/shard_map/jit(cholesky)/cholesky | solution.py:14
  342.1 0.6 compare_reduce_fusion
  342.7 0.6 fusion.26
  343.3 4.9 %custom-call.17 = f32[1,64,64]{1,2,0:T(8,128)S(1)} custom-call(f32[1,64,64]{2,1,0:T(8,128)S(1)} %fusion.26), custom_call_target="InvertDiagBlocksLowerTriangular" | custom-call | tf_op jit(solution)/shard_map/jit(_cho_solve)/triangular_solve | solution.py:15
  348.2 1.2 fusion.29
  349.5 0.3 fusion.27
  349.7 5.6 %all_gather.7 = f32[64,1024]{1,0:T(8,128)S(1)} all-gather(f32[64,512]{1,0:T(8,128)S(1)} %fusion.27), channel_id=1, replica_groups=mesh['samp'=16,'var'=2] {'var'}, dimensions={1}, use_global_device_ids=true | all-gather | bytes 393216 | tf_op jit(solution)/shard_map/all_gather | solution.py:37
  355.4 0.7 copy.23
  (21 shorter events, 0.6 us)
Async XLA Ops:
  7.2 117.1 %all-reduce.3.cloned.1.call-start = ((), (), s32[]{:S(2)}) async-start(), calls=%async_computation.2 | async-start | bytes 6356992 | tf_op jit(solution)/shard_map/psum | solution.py:27
  17.2 159.1 %reduce-scatter.3.cloned.1.call-start = ((), (), s32[]{:S(2)}) async-start(), calls=%async_computation.3 | async-start | bytes 393216 | tf_op jit(solution)/shard_map/reduce_scatter | solution.py:34
  163.7 132.9 %all-reduce.5.cloned.1.call-start = ((), (), s32[]{:S(2)}) async-start(), calls=%async_computation.4 | async-start | bytes 6356992 | tf_op jit(solution)/shard_map/psum | solution.py:27
  193.6 154.6 %reduce-scatter.5.cloned.1.call-start = ((), (), s32[]{:S(2)}) async-start(), calls=%async_computation.5 | async-start | bytes 393216 | tf_op jit(solution)/shard_map/reduce_scatter | solution.py:34
  317.2 10.6 %copy-start = (f32[64,6144]{1,0:T(8,128)}, f32[64,6144]{1,0:T(8,128)S(1)}, u32[]{:S(2)}) copy-start(f32[64,6144]{1,0:T(8,128)S(1)} %fusion.32) | copy-start | bytes 4718596
Sparse Core Ops, SparseCore 0:
  17.3 106.9 all-reduce.2
  163.9 10.4 reduce-scatter.2
  193.8 102.8 all-reduce.4
  336.3 10.3 reduce-scatter.4
where the time goes:
time: 363 us
  waiting for transfers between devices  210 us (58%)
  other arithmetic  55.1 us (15%)
  matrix products  54.1 us (15%)
  blocking collectives  27.9 us (8%)
  between operations  14 us (4%)
    psum x2, waiting for transfers between devices, body(): summed = lax.psum(jnp.concatenate([cross_part, gram_part], axis=1), 'samp')  210 us
    another operation x12, other arithmetic, gram_solve(): factor_low = jnp.linalg.cholesky(gram_matrix + ridge_term * eye_matrix)  26.1 us
    another operation x8, other arithmetic, gram_solve(): return jax.scipy.linalg.cho_solve((factor_low, True), right_side)  22.1 us
    dot_general x2, matrix products, body(): lax.dot_general(freq_b, halved, (((1,), (1,)), ((), ())), preferred_eleme...  18.4 us
    psum x2, blocking collectives, body(): gram_p = lax.psum(pgram_part, 'var')  16.6 us
    another operation x8, matrix products, gram_solve(): return jax.scipy.linalg.cho_solve((factor_low, True), right_side)  16.6 us
    dot_general x2, matrix products, body(): cross_part = jnp.dot(ancestry_b, halved, preferred_element_type=jnp.float32)  14.5 us
    all_gather x2, blocking collectives, body(): ancestry = lax.all_gather(ancestry_share, 'var', axis=1, tiled=True)  11.3 us
  transfers between devices with their start and end apart: 4, of which 2 were waited for; matrix products, arithmetic and copies ran while one was open for 7% of the time, Pallas kernels for 0%

commit v1 on v0

v1 whole, which is shorter than its diff:
```python
import functools

import jax
import jax.numpy as jnp
from jax import lax
from jax.experimental import pallas as pl
from jax.experimental.pallas import tpu as pltpu
from jax.sharding import PartitionSpec as P

ITERS = 2
RIDGE = 1.0
HIGHEST = lax.Precision.HIGHEST


def split_samp(n):
    core = 2 if n % 2 == 0 else 1
    rest = n // core
    inner = max(d for d in range(1, rest + 1) if rest % d == 0 and d * d <= rest)
    return rest // inner, inner, core


def shift_perm(sizes, stage, shift):
    nz, nx, nc = sizes
    pairs = []
    for z in range(nz):
        for x in range(nx):
            for c in range(nc):
                to = [z, x, c]
                to[stage] = (to[stage] + shift) % sizes[stage]
                pairs.append(((z * nx + x) * nc + c, (to[0] * nx + to[1]) * nc + to[2]))
    return pairs


def cross_kernel(nz, n_extra, pos_ref, anc_ref, geno_ref, *refs):
    extra, out_ref, acc_ref = refs[:n_extra], refs[n_extra], refs[n_extra + 1]
    step = pl.program_id(0)
    part = jnp.dot(
        anc_ref[...].astype(jnp.bfloat16), geno_ref[...], preferred_element_type=jnp.float32
    )

    @pl.when(step == 0)
    def _():
        acc_ref[...] = part

    @pl.when(step > 0)
    def _():
        acc_ref[...] += part

    @pl.when(step == pl.num_programs(0) - 1)
    def _():
        chunk = out_ref.shape[2]
        for z in range(nz):
            rel = lax.rem(z - pos_ref[1] + nz, nz)
            value = acc_ref[:, z * chunk : (z + 1) * chunk] * 0.5
            for ref in extra:
                value += ref[rel]
            out_ref[rel] = value


def cross_part(ancestry, genotypes, group, z, nz, groups, extra=()):
    pops, samples = ancestry.shape
    width = genotypes.shape[1] // groups
    chunk = width // nz
    if chunk % 128 or samples % 512:
        part = jnp.dot(
            ancestry.astype(jnp.bfloat16),
            lax.dynamic_slice_in_dim(genotypes, group * width, width, 1),
            preferred_element_type=jnp.float32,
        )
        part = jnp.transpose((part * 0.5).reshape(pops, nz, chunk), (1, 0, 2))
        part = jnp.roll(part, -z, axis=0)
        return functools.reduce(jnp.add, extra, part)
    rows = samples // 4
    whole = pl.BlockSpec((nz, pops, chunk), lambda k, pos: (0, 0, 0))
    return pl.pallas_call(
        functools.partial(cross_kernel, nz, len(extra)),
        out_shape=jax.ShapeDtypeStruct((nz, pops, chunk), jnp.float32),
        grid_spec=pltpu.PrefetchScalarGridSpec(
            num_scalar_prefetch=1,
            grid=(samples // rows,),
            in_specs=[
                pl.BlockSpec((pops, rows), lambda k, pos: (0, k)),
                pl.BlockSpec((rows, width), lambda k, pos: (k, pos[0])),
            ]
            + [whole] * len(extra),
            out_specs=whole,
            scratch_shapes=[pltpu.VMEM((pops, width), jnp.float32)],
        ),
        cost_estimate=pl.CostEstimate(
            flops=2 * pops * samples * width, bytes_accessed=2 * samples * width, transcendentals=0
        ),
        compiler_params=pltpu.CompilerParams(vmem_limit_bytes=16 << 20),
        name="cross_p",
    )(jnp.stack([group, z]).astype(jnp.int32), ancestry, genotypes, *extra)


def fit_kernel(nz, has_acc, pos_ref, freq_ref, geno_ref, *refs):
    if has_acc:
        acc_ref, gacc_ref, out_ref, gram_ref, turned_ref = refs
    else:
        out_ref, gram_ref, turned_ref = refs
    chunk = freq_ref.shape[2]

    @pl.when(pl.program_id(0) == 0)
    def _():
        gram = gacc_ref[...] if has_acc else jnp.zeros(gram_ref.shape, jnp.float32)
        for rel in range(nz):
            value = freq_ref[rel]
            row = lax.rem(rel + pos_ref[1], nz) * chunk
            turned_ref[pl.ds(pl.multiple_of(row, chunk), chunk), :] = value.T.astype(jnp.bfloat16)
            gram += lax.dot_general(
                value, value, (((1,), (1,)), ((), ())), precision=HIGHEST,
                preferred_element_type=jnp.float32,
            )
        gram_ref[...] = gram

    part = jnp.dot(geno_ref[...], turned_ref[...], preferred_element_type=jnp.float32)
    value = part.T * 0.5
    out_ref[...] = acc_ref[...] + value if has_acc else value


def fit_part(freq, genotypes, group, z, groups, acc):
    nz, pops, chunk = freq.shape
    width = nz * chunk
    samples = genotypes.shape[0]
    if chunk % 128 or samples % 512:
        flat = jnp.transpose(jnp.roll(freq, z, axis=0), (1, 0, 2)).reshape(pops, width)
        cross = lax.dot_general(
            flat.astype(jnp.bfloat16),
            lax.dynamic_slice_in_dim(genotypes, group * width, width, 1),
            (((1,), (1,)), ((), ())),
            preferred_element_type=jnp.float32,
        )
        gram = jnp.dot(flat, flat.T, precision=HIGHEST)
        return (cross * 0.5, gram) if acc is None else (acc[0] + cross * 0.5, acc[1] + gram)
    rows = samples // 4
    out_specs = [
        pl.BlockSpec((pops, rows), lambda k, pos: (0, k)),
        pl.BlockSpec((pops, pops), lambda k, pos: (0, 0)),
    ]
    return pl.pallas_call(
        functools.partial(fit_kernel, nz, acc is not None),
        out_shape=[
            jax.ShapeDtypeStruct((pops, samples), jnp.float32),
            jax.ShapeDtypeStruct((pops, pops), jnp.float32),
        ],
        grid_spec=pltpu.PrefetchScalarGridSpec(
            num_scalar_prefetch=1,
            grid=(samples // rows,),
            in_specs=[
                pl.BlockSpec((nz, pops, chunk), lambda k, pos: (0, 0, 0)),
                pl.BlockSpec((rows, width), lambda k, pos: (k, pos[0])),
            ]
            + (out_specs if acc is not None else []),
            out_specs=out_specs,
            scratch_shapes=[pltpu.VMEM((width, pops), jnp.bfloat16)],
        ),
        cost_estimate=pl.CostEstimate(
            flops=2 * pops * samples * width, bytes_accessed=2 * samples * width, transcendentals=0
        ),
        compiler_params=pltpu.CompilerParams(vmem_limit_bytes=16 << 20),
        name="cross_q",
    )(jnp.stack([group, z]).astype(jnp.int32), freq, genotypes, *(acc or ()))


def inverse_kernel(*refs):
    *parts, out_ref = refs
    n = out_ref.shape[0]
    row_id = lax.broadcasted_iota(jnp.int32, (n, n), 0)
    col_id = lax.broadcasted_iota(jnp.int32, (n, n), 1)
    lane = lax.broadcasted_iota(jnp.int32, (1, n), 1)
    sub = lax.broadcasted_iota(jnp.int32, (n, 1), 0)
    a = parts[0][...]
    for ref in parts[1:]:
        a += ref[...]
    a += jnp.where(row_id == col_id, jnp.float32(RIDGE), jnp.float32(0))
    for k in range(n):
        pivot = 1.0 / a[k : k + 1, k : k + 1]
        row = jnp.where(lane == k, 1.0, a[k : k + 1, :]) * pivot
        col = jnp.where(sub == k, -1.0, a[:, k : k + 1])
        a = jnp.where((row_id == k) | (col_id == k), 0.0, a) - col * row
    out_ref[...] = a


def inverse(*parts):
    return pl.pallas_call(
        inverse_kernel,
        out_shape=jax.ShapeDtypeStruct(parts[0].shape, jnp.float32),
        cost_estimate=pl.CostEstimate(flops=1 << 23, bytes_accessed=1 << 22, transcendentals=64),
        compiler_params=pltpu.CompilerParams(vmem_limit_bytes=4 << 20),
        name="inverse",
    )(*parts)


def apply_kernel(inv_ref, *refs):
    *parts, out_ref = refs
    value = parts[0][...]
    for ref in parts[1:]:
        value += ref[...]
    out_ref[...] = jnp.dot(
        inv_ref[...], value, precision=HIGHEST, preferred_element_type=jnp.float32
    )


def apply_inverse(inv, *parts):
    return pl.pallas_call(
        apply_kernel,
        out_shape=jax.ShapeDtypeStruct(parts[0].shape, jnp.float32),
        cost_estimate=pl.CostEstimate(flops=1 << 21, bytes_accessed=1 << 20, transcendentals=0),
        compiler_params=pltpu.CompilerParams(vmem_limit_bytes=8 << 20),
        name="apply",
    )(inv, *parts)


def body(sizes, n_var, genotypes, start_q):
    nz, nx, nc = sizes
    groups = nx * nc
    me = lax.axis_index("samp")
    z, x, c = me // (nx * nc), (me // nc) % nx, me % nc

    def send(value, stage, shift):
        return lax.ppermute(value, "samp", shift_perm(sizes, stage, shift))

    def group_of(rc, rx):
        return (c + rc) % nc * nx + (x + rx) % nx

    def all_sum(value):
        for stage in (2, 1):
            value = functools.reduce(
                jnp.add, [send(value, stage, s) for s in range(1, sizes[stage])], value
            )
        return [value] + [send(value, 0, s) for s in range(1, nz)]

    ancestry = start_q
    for _ in range(ITERS):
        inv_q = inverse(*all_sum(jnp.dot(ancestry, ancestry.T, precision=HIGHEST)))
        order = [*range(1, nx), 0]
        arrived = {
            (rc, rx): send(
                cross_part(ancestry, genotypes, group_of(rc, rx), z, nz, groups), 2, rc
            )
            for rc in range(1, nc)
            for rx in order
        }
        kept = {
            rx: cross_part(
                ancestry, genotypes, group_of(0, rx), z, nz, groups,
                tuple(arrived[rc, rx] for rc in range(1, nc)),
            )
            for rx in order
        }
        mine = [kept[0]] + [send(kept[rx], 1, rx) for rx in range(1, nx)]
        chunks = [functools.reduce(jnp.add, [m[r] for m in mine]) for r in range(nz)]
        total = [chunks[0]] + [send(chunks[r], 0, r) for r in range(1, nz)]
        own = apply_inverse(inv_q, *total)

        held = {(0, 0): jnp.stack([own] + [send(own, 0, -r) for r in range(1, nz)])}
        for rx in range(1, nx):
            held[0, rx] = send(held[0, 0], 1, -rx)
        for rx in range(nx):
            for rc in range(1, nc):
                held[rc, rx] = send(held[0, rx], 2, -rc)

        acc = None
        for (rc, rx), freq in held.items():
            acc = fit_part(freq, genotypes, group_of(rc, rx), z, groups, acc)
        cross_q, gram_p = acc
        if n_var == 2:
            swap = [(0, 1), (1, 0)]
            gram_parts = [gram_p, lax.ppermute(gram_p, "var", swap)]
            cross_parts = [cross_q, lax.ppermute(cross_q, "var", swap)]
        else:
            gram_parts, cross_parts = [lax.psum(gram_p, "var")], [lax.psum(cross_q, "var")]
        ancestry = apply_inverse(inverse(*gram_parts), *cross_parts)

    chunk = own.shape[1]
    frequency = jnp.zeros((own.shape[0], genotypes.shape[1]), jnp.float32)
    for (rc, rx), freq in held.items():
        for r in range(nz):
            at = (group_of(rc, rx) * nz + (z + r) % nz) * chunk
            frequency = lax.dynamic_update_slice(frequency, freq[r], (0, at))
    return (ancestry, frequency)


def solution(mesh):
    sizes = split_samp(mesh.shape["samp"])
    return jax.shard_map(
        functools.partial(body, sizes, mesh.shape["var"]),
        mesh=mesh,
        in_specs=(P("samp", "var"), P(None, "samp")),
        out_specs=(P(None, "samp"), P(None, "var")),
        check_vma=False,
    )
```

time: 363 us -> 194 us (0.53)
  waiting for transfers between devices: 210 us -> 64.3 us
  Pallas kernels: 0 us -> 64.7 us
  other arithmetic: 55.1 us -> 0.47 us
  matrix products: 54.1 us -> 0.71 us
  starting transfers between devices: 0.57 us -> 38.1 us
  blocking collectives: 27.9 us -> 0 us
  local copies, waits for them, and re-layouts: 1.01 us -> 24.2 us
  between operations: 14 us -> 1.24 us
    psum x2 -> x0, waiting for transfers between devices: 210 us -> none  [body(): summed = lax.psum(jnp.concatenate([cross_part, gram_part], axis=1), 'samp')]
    pallas_call x0 -> x24, Pallas kernels: none -> 64.7 us  [the longest x8 24.8 us: fit_part(): pl.pallas_call(functools.partial(fit_kernel, nz, acc is not None), out_sh...]
    ppermute x0 -> x38, waiting for transfers between devices: none -> 64.3 us  [the longest x34 50 us: send(): return lax.ppermute(value, 'samp', shift_perm(sizes, stage, shift))]
    another operation x20 -> x6, other arithmetic: 48.2 us -> 0.35 us  [the longest x3 0.22 us: cross_part(): jnp.stack([group, z]).astype(jnp.int32)]
    ppermute x0 -> x38, starting transfers between devices: none -> 38.1 us  [the longest x34 33.9 us: send(): return lax.ppermute(value, 'samp', shift_perm(sizes, stage, shift))]
    dot_general x8 -> x2, matrix products: 37.5 us -> 0.71 us  [body(): inv_q = inverse(*all_sum(jnp.dot(ancestry, ancestry.T, precision=HIGHEST)))]
    unnamed x3 -> x24, local copies, waits for them, and re-layouts: 0.71 us -> 23.9 us
    psum x2 -> x0, blocking collectives: 16.6 us -> none  [body(): gram_p = lax.psum(pgram_part, 'var')]
  transfers between devices with their start and end apart: 4 -> 38, of which waited for: 2 -> 18; matrix products, arithmetic and copies ran while one was open for 7% -> 1% of each run, Pallas kernels for 0% -> 27%
where the time goes in v1:
time: 194 us
  Pallas kernels  64.7 us (33%)
  waiting for transfers between devices  64.3 us (33%)
  starting transfers between devices  38.1 us (20%)
  local copies, waits for them, and re-layouts  24.2 us (12%)
    ppermute x34, waiting for transfers between devices, send(): return lax.ppermute(value, 'samp', shift_perm(sizes, stage, shift))  50 us
    ppermute x34, starting transfers between devices, send(): return lax.ppermute(value, 'samp', shift_perm(sizes, stage, shift))  33.9 us
    pallas_call x8, Pallas kernels, fit_part(): pl.pallas_call(functools.partial(fit_kernel, nz, acc is not None), out_sh...  24.8 us
    unnamed x24, local copies, waits for them, and re-layouts  23.9 us
    pallas_call x4, Pallas kernels, inverse(): pl.pallas_call(inverse_kernel, out_shape=jax.ShapeDtypeStruct(parts[0].sh...  21.4 us
    pallas_call x8, Pallas kernels, cross_part(): pl.pallas_call(functools.partial(cross_kernel, nz, len(extra)), out_shape...  16.6 us
    ppermute x2, waiting for transfers between devices, body(): gram_parts = [gram_p, lax.ppermute(gram_p, 'var', swap)]  14.2 us
  transfers between devices with their start and end apart: 38, of which 18 were waited for; matrix products, arithmetic and copies ran while one was open for 1% of the time, Pallas kernels for 27%

profile of v1, /device:TPU:0, one launch (start us, length us, event | category | flops | bytes accessed | tf_op | source)
XLA Modules:
  0.0 193.7 jit_solution(9452416656987189518)
XLA Ops:
  0.8 4.6 %copy-done = bf16[1024,6144]{1,0:T(8,128)(2,1)S(1)} copy-done((bf16[1024,6144]{1,0:T(8,128)(2,1)S(1)}, bf16[1024,6144]{1,0:T(8,128)(2,1)}, u32[]{:S(2)}) %copy-start) | copy-done | bytes 12582936
  6.3 2.1 %cross_p.10 = f32[4,64,384]{2,1,0:T(8,128)S(1)} custom-call(s32[2]{0:T(128)S(1)} %pad_add_fusion.pos_ref, f32[64,1024]{1,0:T(8,128)S(1)} %copy-done.6, bf16[1024,6144]{1,0:T(8,128)(2,1)S(1)} %copy-done), custom_call_target="tpu_custom_call" | custom-call | flops 201326592 | bytes 3145728 | tf_op jit(solution)/shard_map/cross_p/pallas_call | solution.py:75
  9.0 4.6 %copy-done.1 = bf16[1024,6144]{1,0:T(8,128)(2,1)S(1)} copy-done((bf16[1024,6144]{1,0:T(8,128)(2,1)S(1)}, bf16[1024,6144]{1,0:T(8,128)(2,1)}, u32[]{:S(2)}) %copy-start.1) | copy-done | bytes 12582936
  13.6 2.1 %cross_p.8 = f32[4,64,384]{2,1,0:T(8,128)S(1)} custom-call(s32[2]{0:T(128)S(1)} %pad_add_fusion.2.pos_ref, f32[64,1024]{1,0:T(8,128)S(1)} %copy-done.7, bf16[1024,6144]{1,0:T(8,128)(2,1)S(1)} %copy-done.1), custom_call_target="tpu_custom_call" | custom-call | flops 201326592 | bytes 3145728 | tf_op jit(solution)/shard_map/cross_p/pallas_call | solution.py:75
  15.9 4.6 %copy-done.2 = bf16[1024,6144]{1,0:T(8,128)(2,1)S(1)} copy-done((bf16[1024,6144]{1,0:T(8,128)(2,1)S(1)}, bf16[1024,6144]{1,0:T(8,128)(2,1)}, u32[]{:S(2)}) %copy-start.2) | copy-done | bytes 12582936
  20.4 2.1 %cross_p.11 = f32[4,64,384]{2,1,0:T(8,128)S(1)} custom-call(s32[2]{0:T(128)S(1)} %pad_add_fusion.3.pos_ref, f32[64,1024]{1,0:T(8,128)S(1)} %copy-done.7, bf16[1024,6144]{1,0:T(8,128)(2,1)S(1)} %copy-done.2, f32[4,64,384]{2,1,0:T(8,128)S(1)} %collective-permute-done.6.refs_0_), custom_call_target="tpu_custom_call" | custom-call | flops 201326592 | bytes 3145728 | tf_op jit(solution)/shard_map/cross_p/pallas_call | solution.py:75
  22.5 3.0 %collective-permute-start.7 = (f32[4,64,384]{2,1,0:T(8,128)S(1)}, f32[4,64,384]{2,1,0:T(8,128)S(1)}, u32[]{:S(2)}, u32[]{:S(2)}) collective-permute-start(f32[4,64,384]{2,1,0:T(8,128)S(1)} %cross_p.11), channel_id=1, source_target_pairs={{0,4},{2,6},{4,0},{6,2},{8,12},{10,14},{12,8},{14,10},{16,20},{18,... | collective-permute-start | bytes 1179656 | tf_op jit(solution)/shard_map/ppermute | solution.py:222
  25.6 4.6 %copy-done.3 = bf16[1024,6144]{1,0:T(8,128)(2,1)S(1)} copy-done((bf16[1024,6144]{1,0:T(8,128)(2,1)S(1)}, bf16[1024,6144]{1,0:T(8,128)(2,1)}, u32[]{:S(2)}) %copy-start.3) | copy-done | bytes 12582936
  30.2 2.1 %cross_p.9 = f32[4,64,384]{2,1,0:T(8,128)S(1)} custom-call(s32[2]{0:T(128)S(1)} %pad_add_fusion.1.pos_ref, f32[64,1024]{1,0:T(8,128)S(1)} %copy-done.7, bf16[1024,6144]{1,0:T(8,128)(2,1)S(1)} %copy-done.3, f32[4,64,384]{2,1,0:T(8,128)S(1)} %collective-permute-done.5.refs_0_), custom_call_target="tpu_custom_call" | custom-call | flops 201326592 | bytes 3145728 | tf_op jit(solution)/shard_map/cross_p/pallas_call | solution.py:75
  32.3 2.6 %collective-permute-done.7 = f32[4,64,384]{2,1,0:T(8,128)S(1)} collective-permute-done((f32[4,64,384]{2,1,0:T(8,128)S(1)}, f32[4,64,384]{2,1,0:T(8,128)S(1)}, u32[]{:S(2)}, u32[]{:S(2)}) %collective-permute-start.7) | collective-permute-done | bytes 393248 | tf_op jit(solution)/shard_map/ppermute | solution.py:222
  34.9 3.9 %collective-permute-start.10 = (f32[64,384]{1,0:T(8,128)S(1)}, f32[64,384]{1,0:T(8,128)S(1)}, u32[]{:S(2)}, u32[]{:S(2)}) collective-permute-start(f32[64,384]{1,0:T(8,128)S(1)} %get-tuple-element.38), channel_id=1, source_target_pairs={{0,24},{2,26},{4,28},{6,30},{8,0},{10,2},{12,4},{14,6},{16,8},{18,... | collective-permute-start | bytes 294920 | tf_op jit(solution)/shard_map/ppermute | solution.py:222
  43.0 2.4 %collective-permute-done.1 = f32[64,64]{1,0:T(8,128)S(1)} collective-permute-done((f32[64,64]{1,0:T(8,128)S(1)}, f32[64,64]{1,0:T(8,128)S(1)}, u32[]{:S(2)}, u32[]{:S(2)}) %collective-permute-start.1) | collective-permute-done | bytes 16416 | tf_op jit(solution)/shard_map/ppermute | solution.py:222
  45.4 3.4 %collective-permute-start.2 = (f32[64,64]{1,0:T(8,128)S(1)}, f32[64,64]{1,0:T(8,128)S(1)}, u32[]{:S(2)}, u32[]{:S(2)}) collective-permute-start(f32[64,64]{1,0:T(8,128)S(1)} %add.361.refs_0_), channel_id=1, source_target_pairs={{0,8},{2,10},{4,12},{6,14},{8,16},{10,18},{12,20},{14,22},{16,24},... | collective-permute-start | bytes 49160 | tf_op jit(solution)/shard_map/ppermute | solution.py:222
  48.8 2.7 %collective-permute-done.2.refs_1_ = f32[64,64]{1,0:T(8,128)S(1)} collective-permute-done((f32[64,64]{1,0:T(8,128)S(1)}, f32[64,64]{1,0:T(8,128)S(1)}, u32[]{:S(2)}, u32[]{:S(2)}) %collective-permute-start.2) | collective-permute-done | bytes 16416 | tf_op jit(solution)/shard_map/ppermute | solution.py:222
  53.6 1.7 collective-permute-done.4.refs_3_
  55.4 5.3 %inverse.4.inv_ref = f32[64,64]{1,0:T(8,128)S(1)} custom-call(f32[64,64]{1,0:T(8,128)S(1)} %add.361.refs_0_, f32[64,64]{1,0:T(8,128)S(1)} %collective-permute-done.2.refs_1_, f32[64,64]{1,0:T(8,128)S(1)} %collective-permute-done.3.refs_2_, f32[64,64]{1,0:T(8,128)S(1)} %collective-permute-done.4.refs_3_), custom_call_target="tpu_custom_call" | custom-call | flops 8388608 | bytes 4194304 | tf_op jit(solution)/shard_map/inverse/pallas_call | solution.py:186
  61.0 2.8 %collective-permute-start.11 = (f32[64,384]{1,0:T(8,128)S(1)}, f32[64,384]{1,0:T(8,128)S(1)}, u32[]{:S(2)}, u32[]{:S(2)}) collective-permute-start(f32[64,384]{1,0:T(8,128)S(1)} %apply.4), channel_id=1, source_target_pairs={{0,24},{2,26},{4,28},{6,30},{8,0},{10,2},{12,4},{14,6},{16,8},{18,... | collective-permute-start | bytes 294920 | tf_op jit(solution)/shard_map/ppermute | solution.py:222
  64.5 2.6 %collective-permute-done.11 = f32[64,384]{1,0:T(8,128)S(1)} collective-permute-done((f32[64,384]{1,0:T(8,128)S(1)}, f32[64,384]{1,0:T(8,128)S(1)}, u32[]{:S(2)}, u32[]{:S(2)}) %collective-permute-start.11) | collective-permute-done | bytes 98336 | tf_op jit(solution)/shard_map/ppermute | solution.py:222
  67.1 3.3 %collective-permute-done.12 = f32[64,384]{1,0:T(8,128)S(1)} collective-permute-done((f32[64,384]{1,0:T(8,128)S(1)}, f32[64,384]{1,0:T(8,128)S(1)}, u32[]{:S(2)}, u32[]{:S(2)}) %collective-permute-start.12) | collective-permute-done | bytes 98336 | tf_op jit(solution)/shard_map/ppermute | solution.py:222
  72.0 6.3 %collective-permute-done.14.freq_ref = f32[4,64,384]{2,1,0:T(8,128)S(1)} collective-permute-done((f32[4,64,384]{2,1,0:T(8,128)S(1)}, f32[4,64,384]{2,1,0:T(8,128)S(1)}, u32[]{:S(2)}, u32[]{:S(2)}) %collective-permute-start.14) | collective-permute-done | bytes 393248 | tf_op jit(solution)/shard_map/ppermute | solution.py:222
  78.3 3.1 %cross_q.8 = (f32[64,1024]{1,0:T(8,128)S(1)}, f32[64,64]{1,0:T(8,128)S(1)}) custom-call(s32[2]{0:T(128)S(1)} %pad_add_fusion.1.pos_ref, f32[4,64,384]{2,1,0:T(8,128)S(1)} %pad_maximum_fusion.freq_ref, bf16[1024,6144]{1,0:T(8,128)(2,1)S(1)} %copy-done.4), custom_call_target="tpu_custom_call" | custom-call | flops 201326592 | bytes 3145728 | tf_op jit(solution)/shard_map/cross_q/pallas_call | solution.py:141
  81.4 3.1 %cross_q.9 = (f32[64,1024]{1,0:T(8,128)S(1)}, f32[64,64]{1,0:T(8,128)S(1)}) custom-call(s32[2]{0:T(128)S(1)} %pad_add_fusion.3.pos_ref, f32[4,64,384]{2,1,0:T(8,128)S(1)} %collective-permute-done.14.freq_ref, bf16[1024,6144]{1,0:T(8,128)(2,1)S(1)} %copy-done.4, f32[64,1024]{1,0:T(8,128)S(1)} %get-tuple-element.18.refs_0_, f32[64,64]{1,0:T(8,128)S(1)} %get-tuple-element.19.refs_1_), custom_call_target="tpu_custom_call" | custom-call | flops 201326592 | bytes 3145728 | tf_op jit(solution)/shard_map/cross_q/pallas_call | solution.py:141
  84.5 3.1 %cross_q.10 = (f32[64,1024]{1,0:T(8,128)S(1)}, f32[64,64]{1,0:T(8,128)S(1)}) custom-call(s32[2]{0:T(128)S(1)} %pad_add_fusion.2.pos_ref, f32[4,64,384]{2,1,0:T(8,128)S(1)} %collective-permute-done.16.freq_ref, bf16[1024,6144]{1,0:T(8,128)(2,1)S(1)} %copy-done.4, f32[64,1024]{1,0:T(8,128)S(1)} %get-tuple-element.20.refs_0_, ...), custom_call_target="tpu_custom_call" | custom-call | flops 201326592 | bytes 3145728 | tf_op jit(solution)/shard_map/cross_q/pallas_call | solution.py:141
  87.6 3.1 %cross_q.11 = (f32[64,1024]{1,0:T(8,128)S(1)}, f32[64,64]{1,0:T(8,128)S(1)}) custom-call(s32[2]{0:T(128)S(1)} %pad_add_fusion.pos_ref, f32[4,64,384]{2,1,0:T(8,128)S(1)} %collective-permute-done.15.freq_ref, bf16[1024,6144]{1,0:T(8,128)(2,1)S(1)} %copy-done.4, f32[64,1024]{1,0:T(8,128)S(1)} %get-tuple-element.22.refs_0_, f32[64,64]{1,0:T(8,128)S(1)} %get-tuple-element.23.refs_1_), custom_call_target="tpu_custom_call" | custom-call | flops 201326592 | bytes 3145728 | tf_op jit(solution)/shard_map/cross_q/pallas_call | solution.py:141
  90.7 1.6 collective-permute-start.18
  92.8 7.4 %collective-permute-done.17.refs_1_ = f32[64,64]{1,0:T(8,128)S(1)} collective-permute-done((f32[64,64]{1,0:T(8,128)S(1)}, f32[64,64]{1,0:T(8,128)S(1)}, u32[]{:S(2)}, u32[]{:S(2)}) %collective-permute-start.17) | collective-permute-done | bytes 16416 | tf_op jit(solution)/shard_map/ppermute | solution.py:270
  100.2 5.3 %inverse.5.inv_ref = f32[64,64]{1,0:T(8,128)S(1)} custom-call(f32[64,64]{1,0:T(8,128)S(1)} %get-tuple-element.24.refs_0_, f32[64,64]{1,0:T(8,128)S(1)} %collective-permute-done.17.refs_1_), custom_call_target="tpu_custom_call" | custom-call | flops 8388608 | bytes 4194304 | tf_op jit(solution)/shard_map/inverse/pallas_call | solution.py:186
  106.0 2.1 %cross_p.14 = f32[4,64,384]{2,1,0:T(8,128)S(1)} custom-call(s32[2]{0:T(128)S(1)} %pad_add_fusion.pos_ref, f32[64,1024]{1,0:T(8,128)S(1)} %apply.5.anc_ref, bf16[1024,6144]{1,0:T(8,128)(2,1)S(1)} %copy-done.4), custom_call_target="tpu_custom_call" | custom-call | flops 201326592 | bytes 3145728 | tf_op jit(solution)/shard_map/cross_p/pallas_call | solution.py:75
  108.2 2.1 %cross_p.12 = f32[4,64,384]{2,1,0:T(8,128)S(1)} custom-call(s32[2]{0:T(128)S(1)} %pad_add_fusion.2.pos_ref, f32[64,1024]{1,0:T(8,128)S(1)} %apply.5.anc_ref, bf16[1024,6144]{1,0:T(8,128)(2,1)S(1)} %copy-done.4), custom_call_target="tpu_custom_call" | custom-call | flops 201326592 | bytes 3145728 | tf_op jit(solution)/shard_map/cross_p/pallas_call | solution.py:75
  110.8 2.1 %cross_p.15 = f32[4,64,384]{2,1,0:T(8,128)S(1)} custom-call(s32[2]{0:T(128)S(1)} %pad_add_fusion.3.pos_ref, f32[64,1024]{1,0:T(8,128)S(1)} %apply.5.anc_ref, bf16[1024,6144]{1,0:T(8,128)(2,1)S(1)} %copy-done.4, f32[4,64,384]{2,1,0:T(8,128)S(1)} %collective-permute-done.25.refs_0_), custom_call_target="tpu_custom_call" | custom-call | flops 201326592 | bytes 3145728 | tf_op jit(solution)/shard_map/cross_p/pallas_call | solution.py:75
  114.5 2.1 %cross_p.13 = f32[4,64,384]{2,1,0:T(8,128)S(1)} custom-call(s32[2]{0:T(128)S(1)} %pad_add_fusion.1.pos_ref, f32[64,1024]{1,0:T(8,128)S(1)} %apply.5.anc_ref, bf16[1024,6144]{1,0:T(8,128)(2,1)S(1)} %copy-done.4, f32[4,64,384]{2,1,0:T(8,128)S(1)} %collective-permute-done.24.refs_0_), custom_call_target="tpu_custom_call" | custom-call | flops 201326592 | bytes 3145728 | tf_op jit(solution)/shard_map/cross_p/pallas_call | solution.py:75
  116.6 7.5 %collective-permute-done.26 = f32[4,64,384]{2,1,0:T(8,128)S(1)} collective-permute-done((f32[4,64,384]{2,1,0:T(8,128)S(1)}, f32[4,64,384]{2,1,0:T(8,128)S(1)}, u32[]{:S(2)}, u32[]{:S(2)}) %collective-permute-start.26) | collective-permute-done | bytes 393248 | tf_op jit(solution)/shard_map/ppermute | solution.py:222
  124.3 1.6 collective-permute-start.28
  125.9 2.5 %collective-permute-start.29 = (f32[64,384]{1,0:T(8,128)S(1)}, f32[64,384]{1,0:T(8,128)S(1)}, u32[]{:S(2)}, u32[]{:S(2)}) collective-permute-start(f32[64,384]{1,0:T(8,128)S(1)} %get-tuple-element.34), channel_id=1, source_target_pairs={{0,24},{2,26},{4,28},{6,30},{8,0},{10,2},{12,4},{14,6},{16,8},{18,... | collective-permute-start | bytes 294920 | tf_op jit(solution)/shard_map/ppermute | solution.py:222
  131.5 2.4 %collective-permute-done.20 = f32[64,64]{1,0:T(8,128)S(1)} collective-permute-done((f32[64,64]{1,0:T(8,128)S(1)}, f32[64,64]{1,0:T(8,128)S(1)}, u32[]{:S(2)}, u32[]{:S(2)}) %collective-permute-start.20) | collective-permute-done | bytes 16416 | tf_op jit(solution)/shard_map/ppermute | solution.py:222
  135.6 4.3 %collective-permute-done.21.refs_1_ = f32[64,64]{1,0:T(8,128)S(1)} collective-permute-done((f32[64,64]{1,0:T(8,128)S(1)}, f32[64,64]{1,0:T(8,128)S(1)}, u32[]{:S(2)}, u32[]{:S(2)}) %collective-permute-start.21) | collective-permute-done | bytes 16416 | tf_op jit(solution)/shard_map/ppermute | solution.py:222
  139.9 3.9 %collective-permute-done.23.refs_3_ = f32[64,64]{1,0:T(8,128)S(1)} collective-permute-done((f32[64,64]{1,0:T(8,128)S(1)}, f32[64,64]{1,0:T(8,128)S(1)}, u32[]{:S(2)}, u32[]{:S(2)}) %collective-permute-start.23) | collective-permute-done | bytes 16416 | tf_op jit(solution)/shard_map/ppermute | solution.py:222
  143.8 5.3 %inverse.6.inv_ref = f32[64,64]{1,0:T(8,128)S(1)} custom-call(f32[64,64]{1,0:T(8,128)S(1)} %add.376.refs_0_, f32[64,64]{1,0:T(8,128)S(1)} %collective-permute-done.21.refs_1_, f32[64,64]{1,0:T(8,128)S(1)} %collective-permute-done.22.refs_2_, f32[64,64]{1,0:T(8,128)S(1)} %collective-permute-done.23.refs_3_), custom_call_target="tpu_custom_call" | custom-call | flops 8388608 | bytes 4194304 | tf_op jit(solution)/shard_map/inverse/pallas_call | solution.py:186
  149.4 1.9 collective-permute-start.30
  151.9 3.5 %collective-permute-done.30 = f32[64,384]{1,0:T(8,128)S(1)} collective-permute-done((f32[64,384]{1,0:T(8,128)S(1)}, f32[64,384]{1,0:T(8,128)S(1)}, u32[]{:S(2)}, u32[]{:S(2)}) %collective-permute-start.30) | collective-permute-done | bytes 98336 | tf_op jit(solution)/shard_map/ppermute | solution.py:222
  155.5 3.1 %collective-permute-done.31 = f32[64,384]{1,0:T(8,128)S(1)} collective-permute-done((f32[64,384]{1,0:T(8,128)S(1)}, f32[64,384]{1,0:T(8,128)S(1)}, u32[]{:S(2)}, u32[]{:S(2)}) %collective-permute-start.31) | collective-permute-done | bytes 98336 | tf_op jit(solution)/shard_map/ppermute | solution.py:222
  160.4 4.6 %copy-done.5 = bf16[1024,6144]{1,0:T(8,128)(2,1)S(1)} copy-done((bf16[1024,6144]{1,0:T(8,128)(2,1)S(1)}, bf16[1024,6144]{1,0:T(8,128)(2,1)}, u32[]{:S(2)}) %copy-start.5) | copy-done | bytes 12582936
  164.9 3.1 %cross_q.12 = (f32[64,1024]{1,0:T(8,128)S(1)}, f32[64,64]{1,0:T(8,128)S(1)}) custom-call(s32[2]{0:T(128)S(1)} %pad_add_fusion.1.pos_ref, f32[4,64,384]{2,1,0:T(8,128)S(1)} %pad_maximum_fusion.1.freq_ref, bf16[1024,6144]{1,0:T(8,128)(2,1)S(1)} %copy-done.5), custom_call_target="tpu_custom_call" | custom-call | flops 201326592 | bytes 3145728 | tf_op jit(solution)/shard_map/cross_q/pallas_call | solution.py:141
  168.8 3.1 %cross_q.13 = (f32[64,1024]{1,0:T(8,128)S(1)}, f32[64,64]{1,0:T(8,128)S(1)}) custom-call(s32[2]{0:T(128)S(1)} %pad_add_fusion.3.pos_ref, f32[4,64,384]{2,1,0:T(8,128)S(1)} %collective-permute-done.33.freq_ref, bf16[1024,6144]{1,0:T(8,128)(2,1)S(1)} %copy-done.5, f32[64,1024]{1,0:T(8,128)S(1)} %get-tuple-element.26.refs_0_, ...), custom_call_target="tpu_custom_call" | custom-call | flops 201326592 | bytes 3145728 | tf_op jit(solution)/shard_map/cross_q/pallas_call | solution.py:141
  172.0 3.1 %cross_q.14 = (f32[64,1024]{1,0:T(8,128)S(1)}, f32[64,64]{1,0:T(8,128)S(1)}) custom-call(s32[2]{0:T(128)S(1)} %pad_add_fusion.2.pos_ref, f32[4,64,384]{2,1,0:T(8,128)S(1)} %collective-permute-done.35.freq_ref, bf16[1024,6144]{1,0:T(8,128)(2,1)S(1)} %copy-done.5, f32[64,1024]{1,0:T(8,128)S(1)} %get-tuple-element.28.refs_0_, ...), custom_call_target="tpu_custom_call" | custom-call | flops 201326592 | bytes 3145728 | tf_op jit(solution)/shard_map/cross_q/pallas_call | solution.py:141
  175.2 3.1 %cross_q.15 = (f32[64,1024]{1,0:T(8,128)S(1)}, f32[64,64]{1,0:T(8,128)S(1)}) custom-call(s32[2]{0:T(128)S(1)} %pad_add_fusion.pos_ref, f32[4,64,384]{2,1,0:T(8,128)S(1)} %collective-permute-done.34.freq_ref, bf16[1024,6144]{1,0:T(8,128)(2,1)S(1)} %bitcast.82, f32[64,1024]{1,0:T(8,128)S(1)} %get-tuple-element.30.refs_0_, f32[64,64]{1,0:T(8,128)S(1)} %get-tuple-element.31.refs_1_), custom_call_target="tpu_custom_call" | custom-call | flops 201326592 | bytes 3145728 | tf_op jit(solution)/shard_map/cross_q/pallas_call | solution.py:141
  180.4 6.8 %collective-permute-done.36.refs_1_ = f32[64,64]{1,0:T(8,128)S(1)} collective-permute-done((f32[64,64]{1,0:T(8,128)S(1)}, f32[64,64]{1,0:T(8,128)S(1)}, u32[]{:S(2)}, u32[]{:S(2)}) %collective-permute-start.36) | collective-permute-done | bytes 16416 | tf_op jit(solution)/shard_map/ppermute | solution.py:270
  187.3 5.3 %inverse.7.inv_ref = f32[64,64]{1,0:T(8,128)S(1)} custom-call(f32[64,64]{1,0:T(8,128)S(1)} %get-tuple-element.32.refs_0_, f32[64,64]{1,0:T(8,128)S(1)} %collective-permute-done.36.refs_1_), custom_call_target="tpu_custom_call" | custom-call | flops 8388608 | bytes 4194304 | tf_op jit(solution)/shard_map/inverse/pallas_call | solution.py:186
  (108 shorter events, 25.6 us)
Async XLA Ops:
  0.8 4.6 %copy-start = (bf16[1024,6144]{1,0:T(8,128)(2,1)S(1)}, bf16[1024,6144]{1,0:T(8,128)(2,1)}, u32[]{:S(2)}) copy-start(bf16[1024,6144]{1,0:T(8,128)(2,1)} %geno_ref.31) | copy-start | bytes 37748740
  8.4 7.5 %collective-permute-start.6 = (f32[4,64,384]{2,1,0:T(8,128)S(1)}, f32[4,64,384]{2,1,0:T(8,128)S(1)}, u32[]{:S(2)}, u32[]{:S(2)}) collective-permute-start(f32[4,64,384]{2,1,0:T(8,128)S(1)} %cross_p.10), channel_id=1, source_target_pairs={{0,2},{2,0},{4,6},{6,4},{8,10},{10,8},{12,14},{14,12},{16,18},{18,... | collective-permute-start | bytes 1179656 | tf_op jit(solution)/shard_map/ppermute | solution.py:222
  9.0 4.6 %copy-start.1 = (bf16[1024,6144]{1,0:T(8,128)(2,1)S(1)}, bf16[1024,6144]{1,0:T(8,128)(2,1)}, u32[]{:S(2)}) copy-start(bf16[1024,6144]{1,0:T(8,128)(2,1)} %geno_ref.31) | copy-start | bytes 37748740
  15.7 9.9 %collective-permute-start.5 = (f32[4,64,384]{2,1,0:T(8,128)S(1)}, f32[4,64,384]{2,1,0:T(8,128)S(1)}, u32[]{:S(2)}, u32[]{:S(2)}) collective-permute-start(f32[4,64,384]{2,1,0:T(8,128)S(1)} %cross_p.8), channel_id=1, source_target_pairs={{0,2},{2,0},{4,6},{6,4},{8,10},{10,8},{12,14},{14,12},{16,18},{18,... | collective-permute-start | bytes 1179656 | tf_op jit(solution)/shard_map/ppermute | solution.py:222
  15.9 4.6 %copy-start.2 = (bf16[1024,6144]{1,0:T(8,128)(2,1)S(1)}, bf16[1024,6144]{1,0:T(8,128)(2,1)}, u32[]{:S(2)}) copy-start(bf16[1024,6144]{1,0:T(8,128)(2,1)} %geno_ref.31) | copy-start | bytes 37748740
  22.5 12.3 %collective-permute-start.7 = (f32[4,64,384]{2,1,0:T(8,128)S(1)}, f32[4,64,384]{2,1,0:T(8,128)S(1)}, u32[]{:S(2)}, u32[]{:S(2)}) collective-permute-start(f32[4,64,384]{2,1,0:T(8,128)S(1)} %cross_p.11), channel_id=1, source_target_pairs={{0,4},{2,6},{4,0},{6,2},{8,12},{10,14},{12,8},{14,10},{16,20},{18,... | collective-permute-start | bytes 1179656 | tf_op jit(solution)/shard_map/ppermute | solution.py:222
  25.6 4.6 %copy-start.3 = (bf16[1024,6144]{1,0:T(8,128)(2,1)S(1)}, bf16[1024,6144]{1,0:T(8,128)(2,1)}, u32[]{:S(2)}) copy-start(bf16[1024,6144]{1,0:T(8,128)(2,1)} %geno_ref.31) | copy-start | bytes 37748740
  30.2 48.1 %copy-start.4 = (bf16[1024,6144]{1,0:T(8,128)(2,1)S(1)}, bf16[1024,6144]{1,0:T(8,128)(2,1)}, u32[]{:S(2)}) copy-start(bf16[1024,6144]{1,0:T(8,128)(2,1)} %geno_ref.31) | copy-start | bytes 37748740
  34.9 25.8 %collective-permute-start.10 = (f32[64,384]{1,0:T(8,128)S(1)}, f32[64,384]{1,0:T(8,128)S(1)}, u32[]{:S(2)}, u32[]{:S(2)}) collective-permute-start(f32[64,384]{1,0:T(8,128)S(1)} %get-tuple-element.38), channel_id=1, source_target_pairs={{0,24},{2,26},{4,28},{6,30},{8,0},{10,2},{12,4},{14,6},{16,8},{18,... | collective-permute-start | bytes 294920 | tf_op jit(solution)/shard_map/ppermute | solution.py:222
  38.8 21.9 %collective-permute-start.8 = (f32[64,384]{1,0:T(8,128)S(1)}, f32[64,384]{1,0:T(8,128)S(1)}, u32[]{:S(2)}, u32[]{:S(2)}) collective-permute-start(f32[64,384]{1,0:T(8,128)S(1)} %get-tuple-element.40), channel_id=1, source_target_pairs={{0,8},{2,10},{4,12},{6,14},{8,16},{10,18},{12,20},{14,22},{16,24},... | collective-permute-start | bytes 294920 | tf_op jit(solution)/shard_map/ppermute | solution.py:222
  38.8 22.0 %collective-permute-start.9 = (f32[64,384]{1,0:T(8,128)S(1)}, f32[64,384]{1,0:T(8,128)S(1)}, u32[]{:S(2)}, u32[]{:S(2)}) collective-permute-start(f32[64,384]{1,0:T(8,128)S(1)} %get-tuple-element.39), channel_id=1, source_target_pairs={{0,16},{2,18},{4,20},{6,22},{8,24},{10,26},{12,28},{14,30},{16,0},... | collective-permute-start | bytes 294920 | tf_op jit(solution)/shard_map/ppermute | solution.py:222
  40.2 1.3 collective-permute-start
  41.5 3.9 %collective-permute-start.1 = (f32[64,64]{1,0:T(8,128)S(1)}, f32[64,64]{1,0:T(8,128)S(1)}, u32[]{:S(2)}, u32[]{:S(2)}) collective-permute-start(f32[64,64]{1,0:T(8,128)S(1)} %add.360), channel_id=1, source_target_pairs={{0,4},{2,6},{4,0},{6,2},{8,12},{10,14},{12,8},{14,10},{16,20},{18,... | collective-permute-start | bytes 49160 | tf_op jit(solution)/shard_map/ppermute | solution.py:222
  45.4 6.1 %collective-permute-start.2 = (f32[64,64]{1,0:T(8,128)S(1)}, f32[64,64]{1,0:T(8,128)S(1)}, u32[]{:S(2)}, u32[]{:S(2)}) collective-permute-start(f32[64,64]{1,0:T(8,128)S(1)} %add.361.refs_0_), channel_id=1, source_target_pairs={{0,8},{2,10},{4,12},{6,14},{8,16},{10,18},{12,20},{14,22},{16,24},... | collective-permute-start | bytes 49160 | tf_op jit(solution)/shard_map/ppermute | solution.py:222
  48.8 4.9 %collective-permute-start.3 = (f32[64,64]{1,0:T(8,128)S(1)}, f32[64,64]{1,0:T(8,128)S(1)}, u32[]{:S(2)}, u32[]{:S(2)}) collective-permute-start(f32[64,64]{1,0:T(8,128)S(1)} %add.361.refs_0_), channel_id=1, source_target_pairs={{0,16},{2,18},{4,20},{6,22},{8,24},{10,26},{12,28},{14,30},{16,0},... | collective-permute-start | bytes 49160 | tf_op jit(solution)/shard_map/ppermute | solution.py:222
  51.5 3.9 %collective-permute-start.4 = (f32[64,64]{1,0:T(8,128)S(1)}, f32[64,64]{1,0:T(8,128)S(1)}, u32[]{:S(2)}, u32[]{:S(2)}) collective-permute-start(f32[64,64]{1,0:T(8,128)S(1)} %add.361.refs_0_), channel_id=1, source_target_pairs={{0,24},{2,26},{4,28},{6,30},{8,0},{10,2},{12,4},{14,6},{16,8},{18,... | collective-permute-start | bytes 49160 | tf_op jit(solution)/shard_map/ppermute | solution.py:222
  61.0 6.1 %collective-permute-start.11 = (f32[64,384]{1,0:T(8,128)S(1)}, f32[64,384]{1,0:T(8,128)S(1)}, u32[]{:S(2)}, u32[]{:S(2)}) collective-permute-start(f32[64,384]{1,0:T(8,128)S(1)} %apply.4), channel_id=1, source_target_pairs={{0,24},{2,26},{4,28},{6,30},{8,0},{10,2},{12,4},{14,6},{16,8},{18,... | collective-permute-start | bytes 294920 | tf_op jit(solution)/shard_map/ppermute | solution.py:222
  63.9 6.6 %collective-permute-start.12 = (f32[64,384]{1,0:T(8,128)S(1)}, f32[64,384]{1,0:T(8,128)S(1)}, u32[]{:S(2)}, u32[]{:S(2)}) collective-permute-start(f32[64,384]{1,0:T(8,128)S(1)} %apply.4), channel_id=1, source_target_pairs={{0,16},{2,18},{4,20},{6,22},{8,24},{10,26},{12,28},{14,30},{16,0},... | collective-permute-start | bytes 294920 | tf_op jit(solution)/shard_map/ppermute | solution.py:222
  63.9 6.6 %collective-permute-start.13 = (f32[64,384]{1,0:T(8,128)S(1)}, f32[64,384]{1,0:T(8,128)S(1)}, u32[]{:S(2)}, u32[]{:S(2)}) collective-permute-start(f32[64,384]{1,0:T(8,128)S(1)} %apply.4), channel_id=1, source_target_pairs={{0,8},{2,10},{4,12},{6,14},{8,16},{10,18},{12,20},{14,22},{16,24},... | collective-permute-start | bytes 294920 | tf_op jit(solution)/shard_map/ppermute | solution.py:222
  70.5 7.8 %collective-permute-start.14 = (f32[4,64,384]{2,1,0:T(8,128)S(1)}, f32[4,64,384]{2,1,0:T(8,128)S(1)}, u32[]{:S(2)}, u32[]{:S(2)}) collective-permute-start(f32[4,64,384]{2,1,0:T(8,128)S(1)} %pad_maximum_fusion.freq_ref), channel_id=1, source_target_pairs={{0,4},{2,6},{4,0},{6,2},{8,12},{10,14},{12,8},{14,10},{16,20},{18,... | collective-permute-start | bytes 1179656 | tf_op jit(solution)/shard_map/ppermute | solution.py:222
  72.0 12.5 %collective-permute-start.16 = (f32[4,64,384]{2,1,0:T(8,128)S(1)}, f32[4,64,384]{2,1,0:T(8,128)S(1)}, u32[]{:S(2)}, u32[]{:S(2)}) collective-permute-start(f32[4,64,384]{2,1,0:T(8,128)S(1)} %pad_maximum_fusion.freq_ref), channel_id=1, source_target_pairs={{0,2},{2,0},{4,6},{6,4},{8,10},{10,8},{12,14},{14,12},{16,18},{18,... | collective-permute-start | bytes 1179656 | tf_op jit(solution)/shard_map/ppermute | solution.py:222
  78.3 9.3 %collective-permute-start.15 = (f32[4,64,384]{2,1,0:T(8,128)S(1)}, f32[4,64,384]{2,1,0:T(8,128)S(1)}, u32[]{:S(2)}, u32[]{:S(2)}) collective-permute-start(f32[4,64,384]{2,1,0:T(8,128)S(1)} %collective-permute-done.14.freq_ref), channel_id=1, source_target_pairs={{0,2},{2,0},{4,6},{6,4},{8,10},{10,8},{12,14},{14,12},{16,18},{18,... | collective-permute-start | bytes 1179656 | tf_op jit(solution)/shard_map/ppermute | solution.py:222
  90.7 14.9 %collective-permute-start.18 = (f32[64,1024]{1,0:T(8,128)S(1)}, f32[64,1024]{1,0:T(8,128)S(1)}, u32[]{:S(2)}, u32[]{:S(2)}) collective-permute-start(f32[64,1024]{1,0:T(8,128)S(1)} %get-tuple-element.25.refs_0_), channel_id=1, source_target_pairs={{0,1},{1,0},{2,3},{3,2},{4,5},{5,4},{6,7},{7,6},{8,9},{9,8},{10,11... | collective-permute-start | bytes 786440 | tf_op jit(solution)/shard_map/ppermute | solution.py:271
  92.3 7.9 %collective-permute-start.17 = (f32[64,64]{1,0:T(8,128)S(1)}, f32[64,64]{1,0:T(8,128)S(1)}, u32[]{:S(2)}, u32[]{:S(2)}) collective-permute-start(f32[64,64]{1,0:T(8,128)S(1)} %get-tuple-element.24.refs_0_), channel_id=1, source_target_pairs={{0,1},{1,0},{2,3},{3,2},{4,5},{5,4},{6,7},{7,6},{8,9},{9,8},{10,11... | collective-permute-start | bytes 49160 | tf_op jit(solution)/shard_map/ppermute | solution.py:270
  108.1 2.7 %collective-permute-start.25 = (f32[4,64,384]{2,1,0:T(8,128)S(1)}, f32[4,64,384]{2,1,0:T(8,128)S(1)}, u32[]{:S(2)}, u32[]{:S(2)}) collective-permute-start(f32[4,64,384]{2,1,0:T(8,128)S(1)} %cross_p.14), channel_id=1, source_target_pairs={{0,2},{2,0},{4,6},{6,4},{8,10},{10,8},{12,14},{14,12},{16,18},{18,... | collective-permute-start | bytes 1179656 | tf_op jit(solution)/shard_map/ppermute | solution.py:222
  110.2 4.2 %collective-permute-start.24 = (f32[4,64,384]{2,1,0:T(8,128)S(1)}, f32[4,64,384]{2,1,0:T(8,128)S(1)}, u32[]{:S(2)}, u32[]{:S(2)}) collective-permute-start(f32[4,64,384]{2,1,0:T(8,128)S(1)} %cross_p.12), channel_id=1, source_target_pairs={{0,2},{2,0},{4,6},{6,4},{8,10},{10,8},{12,14},{14,12},{16,18},{18,... | collective-permute-start | bytes 1179656 | tf_op jit(solution)/shard_map/ppermute | solution.py:222
  112.9 11.1 %collective-permute-start.26 = (f32[4,64,384]{2,1,0:T(8,128)S(1)}, f32[4,64,384]{2,1,0:T(8,128)S(1)}, u32[]{:S(2)}, u32[]{:S(2)}) collective-permute-start(f32[4,64,384]{2,1,0:T(8,128)S(1)} %cross_p.15), channel_id=1, source_target_pairs={{0,4},{2,6},{4,0},{6,2},{8,12},{10,14},{12,8},{14,10},{16,20},{18,... | collective-permute-start | bytes 1179656 | tf_op jit(solution)/shard_map/ppermute | solution.py:222
  124.0 25.1 %collective-permute-start.27 = (f32[64,384]{1,0:T(8,128)S(1)}, f32[64,384]{1,0:T(8,128)S(1)}, u32[]{:S(2)}, u32[]{:S(2)}) collective-permute-start(f32[64,384]{1,0:T(8,128)S(1)} %get-tuple-element.36), channel_id=1, source_target_pairs={{0,8},{2,10},{4,12},{6,14},{8,16},{10,18},{12,20},{14,22},{16,24},... | collective-permute-start | bytes 294920 | tf_op jit(solution)/shard_map/ppermute | solution.py:222
  124.3 24.9 %collective-permute-start.28 = (f32[64,384]{1,0:T(8,128)S(1)}, f32[64,384]{1,0:T(8,128)S(1)}, u32[]{:S(2)}, u32[]{:S(2)}) collective-permute-start(f32[64,384]{1,0:T(8,128)S(1)} %get-tuple-element.35), channel_id=1, source_target_pairs={{0,16},{2,18},{4,20},{6,22},{8,24},{10,26},{12,28},{14,30},{16,0},... | collective-permute-start | bytes 294920 | tf_op jit(solution)/shard_map/ppermute | solution.py:222
  125.9 23.3 %collective-permute-start.29 = (f32[64,384]{1,0:T(8,128)S(1)}, f32[64,384]{1,0:T(8,128)S(1)}, u32[]{:S(2)}, u32[]{:S(2)}) collective-permute-start(f32[64,384]{1,0:T(8,128)S(1)} %get-tuple-element.34), channel_id=1, source_target_pairs={{0,24},{2,26},{4,28},{6,30},{8,0},{10,2},{12,4},{14,6},{16,8},{18,... | collective-permute-start | bytes 294920 | tf_op jit(solution)/shard_map/ppermute | solution.py:222
  128.8 1.3 collective-permute-start.19
  130.0 3.9 %collective-permute-start.20 = (f32[64,64]{1,0:T(8,128)S(1)}, f32[64,64]{1,0:T(8,128)S(1)}, u32[]{:S(2)}, u32[]{:S(2)}) collective-permute-start(f32[64,64]{1,0:T(8,128)S(1)} %add.375), channel_id=1, source_target_pairs={{0,4},{2,6},{4,0},{6,2},{8,12},{10,14},{12,8},{14,10},{16,20},{18,... | collective-permute-start | bytes 49160 | tf_op jit(solution)/shard_map/ppermute | solution.py:222
  134.0 5.9 %collective-permute-start.21 = (f32[64,64]{1,0:T(8,128)S(1)}, f32[64,64]{1,0:T(8,128)S(1)}, u32[]{:S(2)}, u32[]{:S(2)}) collective-permute-start(f32[64,64]{1,0:T(8,128)S(1)} %add.376.refs_0_), channel_id=1, source_target_pairs={{0,8},{2,10},{4,12},{6,14},{8,16},{10,18},{12,20},{14,22},{16,24},... | collective-permute-start | bytes 49160 | tf_op jit(solution)/shard_map/ppermute | solution.py:222
  134.1 5.8 %collective-permute-start.22 = (f32[64,64]{1,0:T(8,128)S(1)}, f32[64,64]{1,0:T(8,128)S(1)}, u32[]{:S(2)}, u32[]{:S(2)}) collective-permute-start(f32[64,64]{1,0:T(8,128)S(1)} %add.376.refs_0_), channel_id=1, source_target_pairs={{0,16},{2,18},{4,20},{6,22},{8,24},{10,26},{12,28},{14,30},{16,0},... | collective-permute-start | bytes 49160 | tf_op jit(solution)/shard_map/ppermute | solution.py:222
  139.9 3.9 %collective-permute-start.23 = (f32[64,64]{1,0:T(8,128)S(1)}, f32[64,64]{1,0:T(8,128)S(1)}, u32[]{:S(2)}, u32[]{:S(2)}) collective-permute-start(f32[64,64]{1,0:T(8,128)S(1)} %add.376.refs_0_), channel_id=1, source_target_pairs={{0,24},{2,26},{4,28},{6,30},{8,0},{10,2},{12,4},{14,6},{16,8},{18,... | collective-permute-start | bytes 49160 | tf_op jit(solution)/shard_map/ppermute | solution.py:222
  149.4 6.0 %collective-permute-start.30 = (f32[64,384]{1,0:T(8,128)S(1)}, f32[64,384]{1,0:T(8,128)S(1)}, u32[]{:S(2)}, u32[]{:S(2)}) collective-permute-start(f32[64,384]{1,0:T(8,128)S(1)} %apply.6), channel_id=1, source_target_pairs={{0,24},{2,26},{4,28},{6,30},{8,0},{10,2},{12,4},{14,6},{16,8},{18,... | collective-permute-start | bytes 294920 | tf_op jit(solution)/shard_map/ppermute | solution.py:222
  151.3 7.3 %collective-permute-start.31 = (f32[64,384]{1,0:T(8,128)S(1)}, f32[64,384]{1,0:T(8,128)S(1)}, u32[]{:S(2)}, u32[]{:S(2)}) collective-permute-start(f32[64,384]{1,0:T(8,128)S(1)} %apply.6), channel_id=1, source_target_pairs={{0,16},{2,18},{4,20},{6,22},{8,24},{10,26},{12,28},{14,30},{16,0},... | collective-permute-start | bytes 294920 | tf_op jit(solution)/shard_map/ppermute | solution.py:222
  151.3 7.3 %collective-permute-start.32 = (f32[64,384]{1,0:T(8,128)S(1)}, f32[64,384]{1,0:T(8,128)S(1)}, u32[]{:S(2)}, u32[]{:S(2)}) collective-permute-start(f32[64,384]{1,0:T(8,128)S(1)} %apply.6), channel_id=1, source_target_pairs={{0,8},{2,10},{4,12},{6,14},{8,16},{10,18},{12,20},{14,22},{16,24},... | collective-permute-start | bytes 294920 | tf_op jit(solution)/shard_map/ppermute | solution.py:222
  158.6 9.5 %collective-permute-start.33 = (f32[4,64,384]{2,1,0:T(8,128)S(1)}, f32[4,64,384]{2,1,0:T(8,128)S(1)}, u32[]{:S(2)}, u32[]{:S(2)}) collective-permute-start(f32[4,64,384]{2,1,0:T(8,128)S(1)} %pad_maximum_fusion.1.freq_ref), channel_id=1, source_target_pairs={{0,4},{2,6},{4,0},{6,2},{8,12},{10,14},{12,8},{14,10},{16,20},{18,... | collective-permute-start | bytes 1179656 | tf_op jit(solution)/shard_map/ppermute | solution.py:222
  160.3 8.5 %collective-permute-start.35 = (f32[4,64,384]{2,1,0:T(8,128)S(1)}, f32[4,64,384]{2,1,0:T(8,128)S(1)}, u32[]{:S(2)}, u32[]{:S(2)}) collective-permute-start(f32[4,64,384]{2,1,0:T(8,128)S(1)} %pad_maximum_fusion.1.freq_ref), channel_id=1, source_target_pairs={{0,2},{2,0},{4,6},{6,4},{8,10},{10,8},{12,14},{14,12},{16,18},{18,... | collective-permute-start | bytes 1179656 | tf_op jit(solution)/shard_map/ppermute | solution.py:222
  160.4 4.6 %copy-start.5 = (bf16[1024,6144]{1,0:T(8,128)(2,1)S(1)}, bf16[1024,6144]{1,0:T(8,128)(2,1)}, u32[]{:S(2)}) copy-start(bf16[1024,6144]{1,0:T(8,128)(2,1)} %geno_ref.31) | copy-start | bytes 37748740
  168.1 7.0 %collective-permute-start.34 = (f32[4,64,384]{2,1,0:T(8,128)S(1)}, f32[4,64,384]{2,1,0:T(8,128)S(1)}, u32[]{:S(2)}, u32[]{:S(2)}) collective-permute-start(f32[4,64,384]{2,1,0:T(8,128)S(1)} %collective-permute-done.33.freq_ref), channel_id=1, source_target_pairs={{0,2},{2,0},{4,6},{6,4},{8,10},{10,8},{12,14},{14,12},{16,18},{18,... | collective-permute-start | bytes 1179656 | tf_op jit(solution)/shard_map/ppermute | solution.py:222
  168.8 6.3 %slice-start = ((s8[12582912]{0:T(1024)(128)(4,1)}), s8[4194304]{0:T(1024)(128)(4,1)S(1)}, s32[]{:S(2)}) async-start(s8[12582912]{0:T(1024)(128)(4,1)} %bitcast.81), calls=%async_computation | async-start | bytes 8388608
  168.8 6.3 %slice-start.1 = ((s8[12582912]{0:T(1024)(128)(4,1)}), s8[4194304]{0:T(1024)(128)(4,1)S(1)}, s32[]{:S(2)}) async-start(s8[12582912]{0:T(1024)(128)(4,1)} %bitcast.81), calls=%async_computation.1 | async-start | bytes 8388608
  171.9 3.2 %slice-start.2 = ((s8[12582912]{0:T(1024)(128)(4,1)}), s8[4194304]{0:T(1024)(128)(4,1)S(1)}, s32[]{:S(2)}) async-start(s8[12582912]{0:T(1024)(128)(4,1)} %bitcast.81), calls=%async_computation.2 | async-start | bytes 8388608
  178.3 14.4 %collective-permute-start.37 = (f32[64,1024]{1,0:T(8,128)S(1)}, f32[64,1024]{1,0:T(8,128)S(1)}, u32[]{:S(2)}, u32[]{:S(2)}) collective-permute-start(f32[64,1024]{1,0:T(8,128)S(1)} %get-tuple-element.33.refs_0_), channel_id=1, source_target_pairs={{0,1},{1,0},{2,3},{3,2},{4,5},{5,4},{6,7},{7,6},{8,9},{9,8},{10,11... | collective-permute-start | bytes 786440 | tf_op jit(solution)/shard_map/ppermute | solution.py:271
  179.8 7.4 %collective-permute-start.36 = (f32[64,64]{1,0:T(8,128)S(1)}, f32[64,64]{1,0:T(8,128)S(1)}, u32[]{:S(2)}, u32[]{:S(2)}) collective-permute-start(f32[64,64]{1,0:T(8,128)S(1)} %get-tuple-element.32.refs_0_), channel_id=1, source_target_pairs={{0,1},{1,0},{2,3},{3,2},{4,5},{5,4},{6,7},{7,6},{8,9},{9,8},{10,11... | collective-permute-start | bytes 49160 | tf_op jit(solution)/shard_map/ppermute | solution.py:270
  180.4 13.3 %copy-start.8 = (f32[64,6144]{1,0:T(8,128)}, f32[64,6144]{1,0:T(8,128)S(1)}, u32[]{:S(2)}) copy-start(f32[64,6144]{1,0:T(8,128)S(1)} %fusion) | copy-start | bytes 4718596
  (2 other events, 3.7 us)

commit v2 on v1

v2 whole, which is shorter than its diff:
```python
import functools

import jax
import jax.numpy as jnp
from jax import lax
from jax.experimental import pallas as pl
from jax.experimental.pallas import tpu as pltpu
from jax.sharding import PartitionSpec as P


ITERS = 2
RIDGE = 1.0
HIGHEST = lax.Precision.HIGHEST


def split_samp(n):
    core = 2 if n % 2 == 0 else 1
    rest = n // core
    inner = max(d for d in range(1, rest + 1) if rest % d == 0 and d * d <= rest)
    return rest // inner, inner, core


def shift_perm(sizes, stage, shift):
    nz, nx, nc = sizes
    pairs = []
    for z in range(nz):
        for x in range(nx):
            for c in range(nc):
                to = [z, x, c]
                to[stage] = (to[stage] + shift) % sizes[stage]
                pairs.append(((z * nx + x) * nc + c, (to[0] * nx + to[1]) * nc + to[2]))
    return pairs


def params(mib):
    return pltpu.CompilerParams(vmem_limit_bytes=mib << 20)


def cost(flops, read):
    return pl.CostEstimate(flops=flops, bytes_accessed=read, transcendentals=0)


VMEM = pl.BlockSpec(memory_space=pltpu.VMEM)
SMEM = pl.BlockSpec(memory_space=pltpu.SMEM)


def gram_of(value):
    high = value.astype(jnp.bfloat16)
    rest = value - high.astype(jnp.float32)
    middle = rest.astype(jnp.bfloat16)
    low = (rest - middle.astype(jnp.float32)).astype(jnp.bfloat16)
    pieces = jnp.concatenate([high, middle, low], axis=0)
    product = lax.dot_general(
        pieces, pieces, (((1,), (1,)), ((), ())), preferred_element_type=jnp.float32
    )
    n = value.shape[0]
    rows = product[2 * n :] + product[n : 2 * n] + product[:n]
    return rows[:, 2 * n :] + rows[:, n : 2 * n] + rows[:, :n]


def gram_kernel(value_ref, *refs):
    out_ref = refs[-1]
    if len(value_ref.shape) == 2:
        total = gram_of(value_ref[...])
    else:
        total = gram_of(jnp.concatenate([value_ref[r] for r in range(value_ref.shape[0])], axis=1))
    for ref in refs[:-1]:
        total += ref[...]
    out_ref[...] = total


def gram(value, *extra):
    pops, width = value.shape[-2:]
    if width % 128:
        flat = value if value.ndim == 2 else jnp.concatenate(list(value), axis=1)
        return functools.reduce(jnp.add, extra, jnp.dot(flat, flat.T, precision=HIGHEST))
    return pl.pallas_call(
        gram_kernel,
        out_shape=jax.ShapeDtypeStruct((pops, pops), jnp.float32),
        in_specs=[VMEM] * (1 + len(extra)),
        out_specs=VMEM,
        cost_estimate=cost(1 << 26, 1 << 20),
        compiler_params=params(8),
        name="gram",
    )(value, *extra)


def store_chunks(out_ref, value, z, nz, chunk, extra):
    for k in range(nz):
        rel = lax.rem(k - z + nz, nz)
        part = value[:, k * chunk : (k + 1) * chunk] * 0.5
        for ref in extra:
            part += ref[rel]
        out_ref[rel] = part


def cross_stream_kernel(nz, n_extra, pos_ref, anc_ref, geno_ref, *refs):
    extra, out_ref, acc_ref = refs[:n_extra], refs[n_extra], refs[n_extra + 1]
    step = pl.program_id(0)
    part = jnp.dot(
        anc_ref[...].astype(jnp.bfloat16), geno_ref[...], preferred_element_type=jnp.float32
    )

    @pl.when(step == 0)
    def _():
        acc_ref[...] = part

    @pl.when(step > 0)
    def _():
        acc_ref[...] += part

    @pl.when(step == pl.num_programs(0) - 1)
    def _():
        store_chunks(out_ref, acc_ref, pos_ref[0], nz, out_ref.shape[2], extra)


def cross_kernel(nz, at, n_extra, pos_ref, anc_ref, geno_ref, *refs):
    extra, out_ref = refs[:n_extra], refs[n_extra]
    chunk = out_ref.shape[2]
    width = nz * chunk
    ancestry_b = anc_ref[...].astype(jnp.bfloat16)
    first = pl.multiple_of(pos_ref[at] * width, 128)
    value = jnp.dot(
        ancestry_b, geno_ref[:, pl.ds(first, width)], preferred_element_type=jnp.float32
    )
    store_chunks(out_ref, value, pos_ref[0], nz, chunk, extra)


def aligned(chunk, samples):
    return chunk % 128 == 0 and samples % 512 == 0


def cross_part(ancestry, genotypes, pos, at, nz, groups, stream, extra=()):
    pops, samples = ancestry.shape
    width = genotypes.shape[1] // groups
    chunk = width // nz
    if not aligned(chunk, samples):
        part = jnp.dot(
            ancestry.astype(jnp.bfloat16),
            lax.dynamic_slice_in_dim(genotypes, pos[at] * width, width, 1),
            preferred_element_type=jnp.float32,
        )
        part = jnp.transpose((part * 0.5).reshape(pops, nz, chunk), (1, 0, 2))
        part = jnp.roll(part, -pos[0], axis=0)
        return functools.reduce(jnp.add, extra, part)
    out_shape = jax.ShapeDtypeStruct((nz, pops, chunk), jnp.float32)
    estimate = cost(2 * pops * samples * width, 2 * samples * width)
    if not stream:
        return pl.pallas_call(
            functools.partial(cross_kernel, nz, at, len(extra)),
            out_shape=out_shape,
            in_specs=[SMEM] + [VMEM] * (2 + len(extra)),
            out_specs=VMEM,
            cost_estimate=estimate,
            compiler_params=params(8),
            name="cross_p",
        )(pos, ancestry, genotypes, *extra)
    rows = samples // 4
    whole = pl.BlockSpec((nz, pops, chunk), lambda k, pos: (0, 0, 0))
    return pl.pallas_call(
        functools.partial(cross_stream_kernel, nz, len(extra)),
        out_shape=out_shape,
        grid_spec=pltpu.PrefetchScalarGridSpec(
            num_scalar_prefetch=1,
            grid=(samples // rows,),
            in_specs=[
                pl.BlockSpec((pops, rows), lambda k, pos: (0, k)),
                pl.BlockSpec((rows, width), lambda k, pos: (k, pos[at])),
            ]
            + [whole] * len(extra),
            out_specs=whole,
            scratch_shapes=[pltpu.VMEM((pops, width), jnp.float32)],
        ),
        cost_estimate=estimate,
        compiler_params=params(56),
        name="cross_p_stream",
    )(pos, ancestry, genotypes, *extra)


def fit_kernel(at, has_acc, last, pos_ref, freq_ref, geno_ref, *refs):
    out_ref, turned_ref = refs[-2:]
    nz, _, chunk = freq_ref.shape
    width = nz * chunk
    for rel in range(nz):
        row = lax.rem(rel + pos_ref[0], nz) * chunk
        turned_ref[pl.ds(pl.multiple_of(row, chunk), chunk), :] = freq_ref[rel].T.astype(
            jnp.bfloat16
        )
    first = pl.multiple_of(pos_ref[at] * width, 128)
    samples = geno_ref.shape[0]
    rows = samples // 4
    for k in range(4):
        part = slice(k * rows, (k + 1) * rows)
        value = 0.5 * jnp.dot(
            geno_ref[part, pl.ds(first, width)], turned_ref[...], preferred_element_type=jnp.float32
        )
        if has_acc:
            value += refs[0][part, :]
        if last:
            out_ref[:, part] = value.T
        else:
            out_ref[part, :] = value


def fit_part(freq, genotypes, pos, at, acc, last):
    nz, pops, chunk = freq.shape
    width = nz * chunk
    samples = genotypes.shape[0]
    if not aligned(chunk, samples):
        flat = jnp.transpose(jnp.roll(freq, pos[0], axis=0), (1, 0, 2)).reshape(pops, width)
        cross = 0.5 * lax.dot_general(
            flat.astype(jnp.bfloat16),
            lax.dynamic_slice_in_dim(genotypes, pos[at] * width, width, 1),
            (((1,), (1,)), ((), ())),
            preferred_element_type=jnp.float32,
        )
        return cross if acc is None else acc + cross
    extra = () if acc is None else (acc,)
    return pl.pallas_call(
        functools.partial(fit_kernel, at, acc is not None, last),
        out_shape=jax.ShapeDtypeStruct((pops, samples) if last else (samples, pops), jnp.float32),
        in_specs=[SMEM] + [VMEM] * (2 + len(extra)),
        out_specs=VMEM,
        scratch_shapes=[pltpu.VMEM((width, pops), jnp.bfloat16)],
        cost_estimate=cost(2 * pops * samples * width, 2 * samples * width),
        compiler_params=params(8),
        name="cross_q",
    )(pos, freq, genotypes, *extra)


def inverse_kernel(*refs):
    *parts, out_ref = refs
    n = out_ref.shape[0]
    row_id = lax.broadcasted_iota(jnp.int32, (n, n), 0)
    col_id = lax.broadcasted_iota(jnp.int32, (n, n), 1)
    lane = lax.broadcasted_iota(jnp.int32, (1, n), 1)
    sub = lax.broadcasted_iota(jnp.int32, (n, 1), 0)
    a = parts[0][...]
    for ref in parts[1:]:
        a += ref[...]
    a += jnp.where(row_id == col_id, jnp.float32(RIDGE), jnp.float32(0))
    for k in range(n):
        pivot = 1.0 / a[k : k + 1, k : k + 1]
        row = jnp.where(lane == k, 1.0, a[k : k + 1, :]) * pivot
        col = jnp.where(sub == k, -1.0, a[:, k : k + 1])
        a = jnp.where((row_id == k) | (col_id == k), 0.0, a) - col * row
    out_ref[...] = a


def inverse(*parts):
    return pl.pallas_call(
        inverse_kernel,
        out_shape=jax.ShapeDtypeStruct(parts[0].shape, jnp.float32),
        in_specs=[VMEM] * len(parts),
        out_specs=VMEM,
        cost_estimate=cost(1 << 28, 1 << 20),
        compiler_params=params(4),
        name="inverse",
    )(*parts)


def apply_kernel(inv_ref, *refs):
    *parts, out_ref = refs
    value = parts[0][...]
    for ref in parts[1:]:
        value += ref[...]
    out_ref[...] = jnp.dot(
        inv_ref[...], value, precision=HIGHEST, preferred_element_type=jnp.float32
    )


def apply_inverse(inv, *parts):
    return pl.pallas_call(
        apply_kernel,
        out_shape=jax.ShapeDtypeStruct(parts[0].shape, jnp.float32),
        in_specs=[VMEM] * (1 + len(parts)),
        out_specs=VMEM,
        cost_estimate=cost(1 << 21, 1 << 20),
        compiler_params=params(8),
        name="apply",
    )(inv, *parts)


def assemble_kernel(places, pos_ref, *refs):
    *held, out_ref = refs
    nz, _, chunk = held[0].shape
    for ref, at in zip(held, places):
        for r in range(nz):
            place = (pos_ref[at] * nz + lax.rem(pos_ref[0] + r, nz)) * chunk
            out_ref[:, pl.ds(pl.multiple_of(place, chunk), chunk)] = ref[r]


def assemble(held, pos, places):
    nz, pops, chunk = held[0].shape
    width = nz * chunk * len(held)
    if chunk % 128:
        frequency = jnp.zeros((pops, width), jnp.float32)
        for freq, at in zip(held, places):
            for r in range(nz):
                place = (pos[at] * nz + (pos[0] + r) % nz) * chunk
                frequency = lax.dynamic_update_slice(frequency, freq[r], (0, place))
        return frequency
    return pl.pallas_call(
        functools.partial(assemble_kernel, places),
        out_shape=jax.ShapeDtypeStruct((pops, width), jnp.float32),
        in_specs=[SMEM] + [VMEM] * len(held),
        out_specs=VMEM,
        cost_estimate=cost(1 << 20, 8 * pops * width),
        compiler_params=params(8),
        name="assemble",
    )(pos, *held)


def body(sizes, n_var, genotypes, start_q):
    nz, nx, nc = sizes
    groups = nx * nc
    me = lax.axis_index("samp")
    z, x, c = me // (nx * nc), (me // nc) % nx, me % nc
    pairs = [(rc, rx) for rx in range(nx) for rc in range(nc)]
    pos = jnp.stack([z] + [(c + rc) % nc * nx + (x + rx) % nx for rc, rx in pairs]).astype(jnp.int32)
    at = {pair: 1 + k for k, pair in enumerate(pairs)}

    def send(value, stage, shift):
        return lax.ppermute(value, "samp", shift_perm(sizes, stage, shift))

    ancestry = start_q
    for it in range(ITERS):
        total = gram(ancestry)
        for stage in (2, 1):
            total = functools.reduce(
                jnp.add, [send(total, stage, s) for s in range(1, sizes[stage])], total
            )
        gram_q = [total] + [send(total, 0, s) for s in range(1, nz)]
        inv_q = inverse(*gram_q)

        order = [*range(1, nx), 0]
        arrived = {}
        for rc in range(1, nc):
            for rx in order:
                part = cross_part(
                    ancestry, genotypes, pos, at[rc, rx], nz,
                    groups, it == 0,
                )
                arrived[rc, rx] = send(part, 2, rc)
        kept = {
            rx: cross_part(
                ancestry, genotypes, pos, at[0, rx], nz, groups,
                it == 0 and rx > 0, tuple(arrived[rc, rx] for rc in range(1, nc)),
            )
            for rx in order
        }
        mine = [kept[0]] + [send(kept[rx], 1, rx) for rx in range(1, nx)]
        chunks = [functools.reduce(jnp.add, [m[r] for m in mine]) for r in range(nz)]
        sums = [chunks[0]] + [send(chunks[r], 0, r) for r in range(1, nz)]
        own = apply_inverse(inv_q, *sums)

        held = {(0, 0): jnp.stack([own] + [send(own, 0, -r) for r in range(1, nz)])}
        for rx in range(1, nx):
            held[0, rx] = send(held[0, 0], 1, -rx)
        for rx in range(nx):
            for rc in range(1, nc):
                held[rc, rx] = send(held[0, rx], 2, -rc)

        gram_p, cross_q = (), None
        for pair in pairs:
            gram_p = (gram(held[pair], *gram_p),)
            cross_q = fit_part(
                held[pair], genotypes, pos, at[pair], cross_q,
                pair == pairs[-1],
            )
        gram_p = gram_p[0]
        if n_var == 2:
            swap = [(0, 1), (1, 0)]
            gram_parts = [gram_p, lax.ppermute(gram_p, "var", swap)]
            cross_parts = [cross_q, lax.ppermute(cross_q, "var", swap)]
        else:
            gram_parts, cross_parts = [lax.psum(gram_p, "var")], [lax.psum(cross_q, "var")]
        inv_p = inverse(*gram_parts)
        ancestry = apply_inverse(inv_p, *cross_parts)
        if it == ITERS - 1:
            frequency = assemble([held[p] for p in pairs], pos, [at[p] for p in pairs])
    return (ancestry, frequency)


def solution(mesh):
    sizes = split_samp(mesh.shape["samp"])
    return jax.shard_map(
        functools.partial(body, sizes, mesh.shape["var"]),
        mesh=mesh,
        in_specs=(P("samp", "var"), P(None, "samp")),
        out_specs=(P(None, "samp"), P(None, "var")),
        check_vma=False,
    )
```

time: 194 us -> 179 us (0.923)
  local copies, waits for them, and re-layouts: 24.2 us -> 10.6 us
    unnamed x24 -> x16, local copies, waits for them, and re-layouts: 23.9 us -> 9.92 us
    ppermute x34, waiting for transfers between devices: 50 us -> 56.4 us  [send(): return lax.ppermute(value, 'samp', shift_perm(sizes, stage, shift))]
    ppermute x2, waiting for transfers between devices: 14.2 us -> 9.54 us  [body(): gram_parts = [gram_p, lax.ppermute(gram_p, 'var', swap)]]
    pallas_call x16 -> x27, Pallas kernels: 41.4 us -> 39.9 us  [the longest x3 14.3 us: cross_part(): pl.pallas_call(functools.partial(cross_stream_kernel, nz, len(extra)), ou...]
  transfers between devices with their start and end apart: 38 -> 38, of which waited for: 18 -> 20; matrix products, arithmetic and copies ran while one was open for 1% -> 0% of each run, Pallas kernels for 27% -> 29%
where the time goes in v2:
time: 179 us
  waiting for transfers between devices  66 us (37%)
  Pallas kernels  63.2 us (35%)
  starting transfers between devices  37.5 us (21%)
  local copies, waits for them, and re-layouts  10.6 us (6%)
    ppermute x34, waiting for transfers between devices, send(): return lax.ppermute(value, 'samp', shift_perm(sizes, stage, shift))  56.4 us
    ppermute x34, starting transfers between devices, send(): return lax.ppermute(value, 'samp', shift_perm(sizes, stage, shift))  33.2 us
    pallas_call x4, Pallas kernels, inverse(): pl.pallas_call(inverse_kernel, out_shape=jax.ShapeDtypeStruct(parts[0].sh...  21.4 us
    pallas_call x3, Pallas kernels, cross_part(): pl.pallas_call(functools.partial(cross_stream_kernel, nz, len(extra)), ou...  14.3 us
    pallas_call x8, Pallas kernels, fit_part(): pl.pallas_call(functools.partial(fit_kernel, at, acc is not None, last),...  13.8 us
    unnamed x16, local copies, waits for them, and re-layouts  9.92 us
    ppermute x2, waiting for transfers between devices, body(): gram_parts = [gram_p, lax.ppermute(gram_p, 'var', swap)]  9.54 us
    pallas_call x5, Pallas kernels, cross_part(): pl.pallas_call(functools.partial(cross_kernel, nz, at, len(extra)), out_s...  6.05 us
  transfers between devices with their start and end apart: 38, of which 20 were waited for; matrix products, arithmetic and copies ran while one was open for 0% of the time, Pallas kernels for 29%

profile of v2, /device:TPU:0, one launch (start us, length us, event | category | flops | bytes accessed | tf_op | source)
XLA Modules:
  0.0 178.6 jit_solution(11171170654819376418)
XLA Ops:
  1.4 4.7 %cross_p_stream.4 = f32[4,64,384]{2,1,0:T(8,128)} custom-call(s32[5]{0:T(128)} %stack.53.pos_ref, f32[64,1024]{1,0:T(8,128)} %anc_ref.7, bf16[1024,6144]{1,0:T(8,128)(2,1)} %geno_ref.31), custom_call_target="tpu_custom_call" | custom-call | flops 201326592 | bytes 3145728 | tf_op jit(solution)/shard_map/cross_p_stream/pallas_call | solution.py:160
  6.6 4.8 %cross_p_stream.3 = f32[4,64,384]{2,1,0:T(8,128)} custom-call(s32[5]{0:T(128)} %stack.53.pos_ref, f32[64,1024]{1,0:T(8,128)} %anc_ref.7, bf16[1024,6144]{1,0:T(8,128)(2,1)} %geno_ref.31), custom_call_target="tpu_custom_call" | custom-call | flops 201326592 | bytes 3145728 | tf_op jit(solution)/shard_map/cross_p_stream/pallas_call | solution.py:160
  12.3 4.9 %cross_p_stream.5 = f32[4,64,384]{2,1,0:T(8,128)} custom-call(s32[5]{0:T(128)} %stack.53.pos_ref, f32[64,1024]{1,0:T(8,128)} %anc_ref.7, bf16[1024,6144]{1,0:T(8,128)(2,1)} %geno_ref.31, f32[4,64,384]{2,1,0:T(8,128)} %copy-done.4), custom_call_target="tpu_custom_call" | custom-call | flops 201326592 | bytes 3145728 | tf_op jit(solution)/shard_map/cross_p_stream/pallas_call | solution.py:160
  17.1 2.8 %collective-permute-start.7 = (f32[4,64,384]{2,1,0:T(8,128)}, f32[4,64,384]{2,1,0:T(8,128)S(1)}, u32[]{:S(2)}, u32[]{:S(2)}) collective-permute-start(f32[4,64,384]{2,1,0:T(8,128)} %cross_p_stream.5), channel_id=1, source_target_pairs={{0,4},{2,6},{4,0},{6,2},{8,12},{10,14},{12,8},{14,10},{16,20},{18,... | collective-permute-start | bytes 1179656 | tf_op jit(solution)/shard_map/ppermute | solution.py:324
  20.0 4.6 %copy-done = bf16[1024,6144]{1,0:T(8,128)(2,1)S(1)} copy-done((bf16[1024,6144]{1,0:T(8,128)(2,1)S(1)}, bf16[1024,6144]{1,0:T(8,128)(2,1)}, u32[]{:S(2)}) %copy-start) | copy-done | bytes 12582936
  25.8 3.8 %collective-permute-done.7 = f32[4,64,384]{2,1,0:T(8,128)S(1)} collective-permute-done((f32[4,64,384]{2,1,0:T(8,128)}, f32[4,64,384]{2,1,0:T(8,128)S(1)}, u32[]{:S(2)}, u32[]{:S(2)}) %collective-permute-start.7) | collective-permute-done | bytes 393248 | tf_op jit(solution)/shard_map/ppermute | solution.py:324
  29.6 1.9 %collective-permute-start.8 = (f32[64,384]{1,0:T(8,128)S(1)}, f32[64,384]{1,0:T(8,128)S(1)}, u32[]{:S(2)}, u32[]{:S(2)}) collective-permute-start(f32[64,384]{1,0:T(8,128)S(1)} %get-tuple-element.8), channel_id=1, source_target_pairs={{0,8},{2,10},{4,12},{6,14},{8,16},{10,18},{12,20},{14,22},{16,24},... | collective-permute-start | bytes 294920 | tf_op jit(solution)/shard_map/ppermute | solution.py:324
  31.5 2.6 %collective-permute-start.9 = (f32[64,384]{1,0:T(8,128)S(1)}, f32[64,384]{1,0:T(8,128)S(1)}, u32[]{:S(2)}, u32[]{:S(2)}) collective-permute-start(f32[64,384]{1,0:T(8,128)S(1)} %get-tuple-element.7), channel_id=1, source_target_pairs={{0,16},{2,18},{4,20},{6,22},{8,24},{10,26},{12,28},{14,30},{16,0},... | collective-permute-start | bytes 294920 | tf_op jit(solution)/shard_map/ppermute | solution.py:324
  37.1 1.5 collective-permute-start.1
  38.6 2.4 %collective-permute-done.1 = f32[64,64]{1,0:T(8,128)S(1)} collective-permute-done((f32[64,64]{1,0:T(8,128)S(1)}, f32[64,64]{1,0:T(8,128)S(1)}, u32[]{:S(2)}, u32[]{:S(2)}) %collective-permute-start.1) | collective-permute-done | bytes 16416 | tf_op jit(solution)/shard_map/ppermute | solution.py:324
  42.0 4.8 %collective-permute-done.2.refs_1_ = f32[64,64]{1,0:T(8,128)S(1)} collective-permute-done((f32[64,64]{1,0:T(8,128)S(1)}, f32[64,64]{1,0:T(8,128)S(1)}, u32[]{:S(2)}, u32[]{:S(2)}) %collective-permute-start.2) | collective-permute-done | bytes 16416 | tf_op jit(solution)/shard_map/ppermute | solution.py:324
  47.5 3.2 %collective-permute-done.4.refs_3_ = f32[64,64]{1,0:T(8,128)S(1)} collective-permute-done((f32[64,64]{1,0:T(8,128)S(1)}, f32[64,64]{1,0:T(8,128)S(1)}, u32[]{:S(2)}, u32[]{:S(2)}) %collective-permute-start.4) | collective-permute-done | bytes 16416 | tf_op jit(solution)/shard_map/ppermute | solution.py:324
  50.7 5.3 %inverse.4.inv_ref = f32[64,64]{1,0:T(8,128)S(1)} custom-call(f32[64,64]{1,0:T(8,128)S(1)} %add.104.refs_0_, f32[64,64]{1,0:T(8,128)S(1)} %collective-permute-done.2.refs_1_, f32[64,64]{1,0:T(8,128)S(1)} %collective-permute-done.3.refs_2_, f32[64,64]{1,0:T(8,128)S(1)} %collective-permute-done.4.refs_3_), custom_call_target="tpu_custom_call" | custom-call | flops 268435456 | bytes 1048576 | tf_op jit(solution)/shard_map/inverse/pallas_call | solution.py:251
  56.4 2.4 %collective-permute-start.12 = (f32[64,384]{1,0:T(8,128)S(1)}, f32[64,384]{1,0:T(8,128)S(1)}, u32[]{:S(2)}, u32[]{:S(2)}) collective-permute-start(f32[64,384]{1,0:T(8,128)S(1)} %apply.4), channel_id=1, source_target_pairs={{0,16},{2,18},{4,20},{6,22},{8,24},{10,26},{12,28},{14,30},{16,0},... | collective-permute-start | bytes 294920 | tf_op jit(solution)/shard_map/ppermute | solution.py:324
  60.3 2.7 %collective-permute-done.13 = f32[64,384]{1,0:T(8,128)S(1)} collective-permute-done((f32[64,384]{1,0:T(8,128)S(1)}, f32[64,384]{1,0:T(8,128)S(1)}, u32[]{:S(2)}, u32[]{:S(2)}) %collective-permute-start.13) | collective-permute-done | bytes 98336 | tf_op jit(solution)/shard_map/ppermute | solution.py:324
  64.4 1.6 collective-permute-start.14
  65.9 6.3 %collective-permute-done.14.value_ref.freq_ref = f32[4,64,384]{2,1,0:T(8,128)S(1)} collective-permute-done((f32[4,64,384]{2,1,0:T(8,128)S(1)}, f32[4,64,384]{2,1,0:T(8,128)S(1)}, u32[]{:S(2)}, u32[]{:S(2)}) %collective-permute-start.14) | collective-permute-done | bytes 393248 | tf_op jit(solution)/shard_map/ppermute | solution.py:324
  72.2 4.6 %copy-done.1 = bf16[1024,6144]{1,0:T(8,128)(2,1)S(1)} copy-done((bf16[1024,6144]{1,0:T(8,128)(2,1)S(1)}, bf16[1024,6144]{1,0:T(8,128)(2,1)}, u32[]{:S(2)}) %copy-start.1) | copy-done | bytes 12582936
  76.8 1.7 cross_q.8.refs_0_
  78.5 1.7 cross_q.9.refs_0_
  80.3 1.7 cross_q.10.refs_0_
  82.0 1.8 cross_q.11.refs_0_
  83.7 1.6 collective-permute-start.18
  87.6 5.7 %collective-permute-done.17.refs_1_ = f32[64,64]{1,0:T(8,128)S(1)} collective-permute-done((f32[64,64]{1,0:T(8,128)S(1)}, f32[64,64]{1,0:T(8,128)S(1)}, u32[]{:S(2)}, u32[]{:S(2)}) %collective-permute-start.17) | collective-permute-done | bytes 16416 | tf_op jit(solution)/shard_map/ppermute | solution.py:374
  93.2 5.3 %inverse.5.inv_ref = f32[64,64]{1,0:T(8,128)S(1)} custom-call(f32[64,64]{1,0:T(8,128)S(1)} %gram.14.refs_0_, f32[64,64]{1,0:T(8,128)S(1)} %collective-permute-done.17.refs_1_), custom_call_target="tpu_custom_call" | custom-call | flops 268435456 | bytes 1048576 | tf_op jit(solution)/shard_map/inverse/pallas_call | solution.py:251
  103.3 1.6 collective-permute-start.26
  106.1 8.4 %collective-permute-done.26 = f32[4,64,384]{2,1,0:T(8,128)S(1)} collective-permute-done((f32[4,64,384]{2,1,0:T(8,128)S(1)}, f32[4,64,384]{2,1,0:T(8,128)S(1)}, u32[]{:S(2)}, u32[]{:S(2)}) %collective-permute-start.26) | collective-permute-done | bytes 393248 | tf_op jit(solution)/shard_map/ppermute | solution.py:324
  114.5 1.7 collective-permute-start.27
  116.2 2.0 %collective-permute-start.28 = (f32[64,384]{1,0:T(8,128)S(1)}, f32[64,384]{1,0:T(8,128)S(1)}, u32[]{:S(2)}, u32[]{:S(2)}) collective-permute-start(f32[64,384]{1,0:T(8,128)S(1)} %get-tuple-element.3), channel_id=1, source_target_pairs={{0,16},{2,18},{4,20},{6,22},{8,24},{10,26},{12,28},{14,30},{16,0},... | collective-permute-start | bytes 294920 | tf_op jit(solution)/shard_map/ppermute | solution.py:324
  120.4 1.5 collective-permute-start.20
  121.9 2.4 %collective-permute-done.20 = f32[64,64]{1,0:T(8,128)S(1)} collective-permute-done((f32[64,64]{1,0:T(8,128)S(1)}, f32[64,64]{1,0:T(8,128)S(1)}, u32[]{:S(2)}, u32[]{:S(2)}) %collective-permute-start.20) | collective-permute-done | bytes 16416 | tf_op jit(solution)/shard_map/ppermute | solution.py:324
  124.3 1.5 collective-permute-start.21
  126.7 3.4 %collective-permute-done.21.refs_1_ = f32[64,64]{1,0:T(8,128)S(1)} collective-permute-done((f32[64,64]{1,0:T(8,128)S(1)}, f32[64,64]{1,0:T(8,128)S(1)}, u32[]{:S(2)}, u32[]{:S(2)}) %collective-permute-start.21) | collective-permute-done | bytes 16416 | tf_op jit(solution)/shard_map/ppermute | solution.py:324
  131.1 3.0 %collective-permute-done.23.refs_3_ = f32[64,64]{1,0:T(8,128)S(1)} collective-permute-done((f32[64,64]{1,0:T(8,128)S(1)}, f32[64,64]{1,0:T(8,128)S(1)}, u32[]{:S(2)}, u32[]{:S(2)}) %collective-permute-start.23) | collective-permute-done | bytes 16416 | tf_op jit(solution)/shard_map/ppermute | solution.py:324
  134.0 5.3 %inverse.6.inv_ref = f32[64,64]{1,0:T(8,128)S(1)} custom-call(f32[64,64]{1,0:T(8,128)S(1)} %add.126.refs_0_, f32[64,64]{1,0:T(8,128)S(1)} %collective-permute-done.21.refs_1_, f32[64,64]{1,0:T(8,128)S(1)} %collective-permute-done.22.refs_2_, f32[64,64]{1,0:T(8,128)S(1)} %collective-permute-done.23.refs_3_), custom_call_target="tpu_custom_call" | custom-call | flops 268435456 | bytes 1048576 | tf_op jit(solution)/shard_map/inverse/pallas_call | solution.py:251
  139.7 2.4 %collective-permute-start.31 = (f32[64,384]{1,0:T(8,128)S(1)}, f32[64,384]{1,0:T(8,128)S(1)}, u32[]{:S(2)}, u32[]{:S(2)}) collective-permute-start(f32[64,384]{1,0:T(8,128)S(1)} %apply.6), channel_id=1, source_target_pairs={{0,16},{2,18},{4,20},{6,22},{8,24},{10,26},{12,28},{14,30},{16,0},... | collective-permute-start | bytes 294920 | tf_op jit(solution)/shard_map/ppermute | solution.py:324
  143.6 2.7 %collective-permute-done.32 = f32[64,384]{1,0:T(8,128)S(1)} collective-permute-done((f32[64,384]{1,0:T(8,128)S(1)}, f32[64,384]{1,0:T(8,128)S(1)}, u32[]{:S(2)}, u32[]{:S(2)}) %collective-permute-start.32) | collective-permute-done | bytes 98336 | tf_op jit(solution)/shard_map/ppermute | solution.py:324
  146.3 1.6 collective-permute-done.31
  147.9 1.6 collective-permute-start.33
  149.5 6.3 %collective-permute-done.33.value_ref.freq_ref.refs_2_ = f32[4,64,384]{2,1,0:T(8,128)S(1)} collective-permute-done((f32[4,64,384]{2,1,0:T(8,128)S(1)}, f32[4,64,384]{2,1,0:T(8,128)S(1)}, u32[]{:S(2)}, u32[]{:S(2)}) %collective-permute-start.33) | collective-permute-done | bytes 393248 | tf_op jit(solution)/shard_map/ppermute | solution.py:324
  155.7 1.7 cross_q.12.refs_0_
  157.5 1.7 cross_q.13.refs_0_
  159.2 1.7 cross_q.14.refs_0_
  160.9 1.8 cross_q.15.refs_0_
  162.7 1.6 collective-permute-start.37
  166.5 1.8 %assemble.1 = f32[64,6144]{1,0:T(8,128)} custom-call(s32[5]{0:T(128)S(1)} %copy-done.3, f32[4,64,384]{2,1,0:T(8,128)S(1)} %pad_maximum_fusion.1.value_ref.freq_ref.refs_0_, f32[4,64,384]{2,1,0:T(8,128)S(1)} %collective-permute-done.35.value_ref.freq_ref.refs_1_, f32[4,64,384]{2,1,0:T(8,128)S(1)} %collective-permute-done.33.value_ref.freq_ref.refs_2_, ...), custom_call_target="tpu_custom_call" | custom-call | flops 1048576 | bytes 3145728 | tf_op jit(solution)/shard_map/assemble/pallas_call | solution.py:303
  168.3 3.9 %collective-permute-done.36.refs_1_ = f32[64,64]{1,0:T(8,128)S(1)} collective-permute-done((f32[64,64]{1,0:T(8,128)S(1)}, f32[64,64]{1,0:T(8,128)S(1)}, u32[]{:S(2)}, u32[]{:S(2)}) %collective-permute-start.36) | collective-permute-done | bytes 16416 | tf_op jit(solution)/shard_map/ppermute | solution.py:374
  172.1 5.3 %inverse.7.inv_ref = f32[64,64]{1,0:T(8,128)S(1)} custom-call(f32[64,64]{1,0:T(8,128)S(1)} %gram.19.refs_0_, f32[64,64]{1,0:T(8,128)S(1)} %collective-permute-done.36.refs_1_), custom_call_target="tpu_custom_call" | custom-call | flops 268435456 | bytes 1048576 | tf_op jit(solution)/shard_map/inverse/pallas_call | solution.py:251
  (89 shorter events, 28.4 us)
Async XLA Ops:
  6.1 13.8 %copy-start.2 = (f32[64,1024]{1,0:T(8,128)S(1)}, f32[64,1024]{1,0:T(8,128)}, u32[]{:S(2)}) copy-start(f32[64,1024]{1,0:T(8,128)} %anc_ref.7) | copy-start | bytes 786436
  6.1 13.8 %copy-start.3 = (s32[5]{0:T(128)S(1)}, s32[5]{0:T(128)}, u32[]{:S(2)}) copy-start(s32[5]{0:T(128)} %stack.53.pos_ref) | copy-start | bytes 64
  6.1 5.4 %collective-permute-start.6 = (f32[4,64,384]{2,1,0:T(8,128)}, f32[4,64,384]{2,1,0:T(8,128)S(1)}, u32[]{:S(2)}, u32[]{:S(2)}) collective-permute-start(f32[4,64,384]{2,1,0:T(8,128)} %cross_p_stream.4), channel_id=1, source_target_pairs={{0,2},{2,0},{4,6},{6,4},{8,10},{10,8},{12,14},{14,12},{16,18},{18,... | collective-permute-start | bytes 1179656 | tf_op jit(solution)/shard_map/ppermute | solution.py:324
  11.4 8.6 %collective-permute-start.5 = (f32[4,64,384]{2,1,0:T(8,128)}, f32[4,64,384]{2,1,0:T(8,128)S(1)}, u32[]{:S(2)}, u32[]{:S(2)}) collective-permute-start(f32[4,64,384]{2,1,0:T(8,128)} %cross_p_stream.3), channel_id=1, source_target_pairs={{0,2},{2,0},{4,6},{6,4},{8,10},{10,8},{12,14},{14,12},{16,18},{18,... | collective-permute-start | bytes 1179656 | tf_op jit(solution)/shard_map/ppermute | solution.py:324
  11.5 0.7 copy-start.4
  17.1 12.5 %collective-permute-start.7 = (f32[4,64,384]{2,1,0:T(8,128)}, f32[4,64,384]{2,1,0:T(8,128)S(1)}, u32[]{:S(2)}, u32[]{:S(2)}) collective-permute-start(f32[4,64,384]{2,1,0:T(8,128)} %cross_p_stream.5), channel_id=1, source_target_pairs={{0,4},{2,6},{4,0},{6,2},{8,12},{10,14},{12,8},{14,10},{16,20},{18,... | collective-permute-start | bytes 1179656 | tf_op jit(solution)/shard_map/ppermute | solution.py:324
  20.0 4.6 %copy-start = (bf16[1024,6144]{1,0:T(8,128)(2,1)S(1)}, bf16[1024,6144]{1,0:T(8,128)(2,1)}, u32[]{:S(2)}) copy-start(bf16[1024,6144]{1,0:T(8,128)(2,1)} %geno_ref.31) | copy-start | bytes 37748740
  29.6 26.5 %collective-permute-start.8 = (f32[64,384]{1,0:T(8,128)S(1)}, f32[64,384]{1,0:T(8,128)S(1)}, u32[]{:S(2)}, u32[]{:S(2)}) collective-permute-start(f32[64,384]{1,0:T(8,128)S(1)} %get-tuple-element.8), channel_id=1, source_target_pairs={{0,8},{2,10},{4,12},{6,14},{8,16},{10,18},{12,20},{14,22},{16,24},... | collective-permute-start | bytes 294920 | tf_op jit(solution)/shard_map/ppermute | solution.py:324
  31.5 24.6 %collective-permute-start.9 = (f32[64,384]{1,0:T(8,128)S(1)}, f32[64,384]{1,0:T(8,128)S(1)}, u32[]{:S(2)}, u32[]{:S(2)}) collective-permute-start(f32[64,384]{1,0:T(8,128)S(1)} %get-tuple-element.7), channel_id=1, source_target_pairs={{0,16},{2,18},{4,20},{6,22},{8,24},{10,26},{12,28},{14,30},{16,0},... | collective-permute-start | bytes 294920 | tf_op jit(solution)/shard_map/ppermute | solution.py:324
  34.1 22.0 %collective-permute-start.10 = (f32[64,384]{1,0:T(8,128)S(1)}, f32[64,384]{1,0:T(8,128)S(1)}, u32[]{:S(2)}, u32[]{:S(2)}) collective-permute-start(f32[64,384]{1,0:T(8,128)S(1)} %get-tuple-element.6), channel_id=1, source_target_pairs={{0,24},{2,26},{4,28},{6,30},{8,0},{10,2},{12,4},{14,6},{16,8},{18,... | collective-permute-start | bytes 294920 | tf_op jit(solution)/shard_map/ppermute | solution.py:324
  35.8 1.3 collective-permute-start
  37.1 3.9 %collective-permute-start.1 = (f32[64,64]{1,0:T(8,128)S(1)}, f32[64,64]{1,0:T(8,128)S(1)}, u32[]{:S(2)}, u32[]{:S(2)}) collective-permute-start(f32[64,64]{1,0:T(8,128)S(1)} %add.103), channel_id=1, source_target_pairs={{0,4},{2,6},{4,0},{6,2},{8,12},{10,14},{12,8},{14,10},{16,20},{18,... | collective-permute-start | bytes 49160 | tf_op jit(solution)/shard_map/ppermute | solution.py:324
  41.0 5.8 %collective-permute-start.2 = (f32[64,64]{1,0:T(8,128)S(1)}, f32[64,64]{1,0:T(8,128)S(1)}, u32[]{:S(2)}, u32[]{:S(2)}) collective-permute-start(f32[64,64]{1,0:T(8,128)S(1)} %add.104.refs_0_), channel_id=1, source_target_pairs={{0,8},{2,10},{4,12},{6,14},{8,16},{10,18},{12,20},{14,22},{16,24},... | collective-permute-start | bytes 49160 | tf_op jit(solution)/shard_map/ppermute | solution.py:324
  41.7 5.8 %collective-permute-start.3 = (f32[64,64]{1,0:T(8,128)S(1)}, f32[64,64]{1,0:T(8,128)S(1)}, u32[]{:S(2)}, u32[]{:S(2)}) collective-permute-start(f32[64,64]{1,0:T(8,128)S(1)} %add.104.refs_0_), channel_id=1, source_target_pairs={{0,16},{2,18},{4,20},{6,22},{8,24},{10,26},{12,28},{14,30},{16,0},... | collective-permute-start | bytes 49160 | tf_op jit(solution)/shard_map/ppermute | solution.py:324
  46.8 3.9 %collective-permute-start.4 = (f32[64,64]{1,0:T(8,128)S(1)}, f32[64,64]{1,0:T(8,128)S(1)}, u32[]{:S(2)}, u32[]{:S(2)}) collective-permute-start(f32[64,64]{1,0:T(8,128)S(1)} %add.104.refs_0_), channel_id=1, source_target_pairs={{0,24},{2,26},{4,28},{6,30},{8,0},{10,2},{12,4},{14,6},{16,8},{18,... | collective-permute-start | bytes 49160 | tf_op jit(solution)/shard_map/ppermute | solution.py:324
  56.4 6.6 %collective-permute-start.13 = (f32[64,384]{1,0:T(8,128)S(1)}, f32[64,384]{1,0:T(8,128)S(1)}, u32[]{:S(2)}, u32[]{:S(2)}) collective-permute-start(f32[64,384]{1,0:T(8,128)S(1)} %apply.4), channel_id=1, source_target_pairs={{0,8},{2,10},{4,12},{6,14},{8,16},{10,18},{12,20},{14,22},{16,24},... | collective-permute-start | bytes 294920 | tf_op jit(solution)/shard_map/ppermute | solution.py:324
  56.4 7.9 %collective-permute-start.12 = (f32[64,384]{1,0:T(8,128)S(1)}, f32[64,384]{1,0:T(8,128)S(1)}, u32[]{:S(2)}, u32[]{:S(2)}) collective-permute-start(f32[64,384]{1,0:T(8,128)S(1)} %apply.4), channel_id=1, source_target_pairs={{0,16},{2,18},{4,20},{6,22},{8,24},{10,26},{12,28},{14,30},{16,0},... | collective-permute-start | bytes 294920 | tf_op jit(solution)/shard_map/ppermute | solution.py:324
  58.8 5.5 %collective-permute-start.11 = (f32[64,384]{1,0:T(8,128)S(1)}, f32[64,384]{1,0:T(8,128)S(1)}, u32[]{:S(2)}, u32[]{:S(2)}) collective-permute-start(f32[64,384]{1,0:T(8,128)S(1)} %apply.4), channel_id=1, source_target_pairs={{0,24},{2,26},{4,28},{6,30},{8,0},{10,2},{12,4},{14,6},{16,8},{18,... | collective-permute-start | bytes 294920 | tf_op jit(solution)/shard_map/ppermute | solution.py:324
  64.4 7.8 %collective-permute-start.14 = (f32[4,64,384]{2,1,0:T(8,128)S(1)}, f32[4,64,384]{2,1,0:T(8,128)S(1)}, u32[]{:S(2)}, u32[]{:S(2)}) collective-permute-start(f32[4,64,384]{2,1,0:T(8,128)S(1)} %pad_maximum_fusion.value_ref.freq_ref), channel_id=1, source_target_pairs={{0,4},{2,6},{4,0},{6,2},{8,12},{10,14},{12,8},{14,10},{16,20},{18,... | collective-permute-start | bytes 1179656 | tf_op jit(solution)/shard_map/ppermute | solution.py:324
  65.9 12.6 %collective-permute-start.16 = (f32[4,64,384]{2,1,0:T(8,128)S(1)}, f32[4,64,384]{2,1,0:T(8,128)S(1)}, u32[]{:S(2)}, u32[]{:S(2)}) collective-permute-start(f32[4,64,384]{2,1,0:T(8,128)S(1)} %pad_maximum_fusion.value_ref.freq_ref), channel_id=1, source_target_pairs={{0,2},{2,0},{4,6},{6,4},{8,10},{10,8},{12,14},{14,12},{16,18},{18,... | collective-permute-start | bytes 1179656 | tf_op jit(solution)/shard_map/ppermute | solution.py:324
  72.2 9.8 %collective-permute-start.15 = (f32[4,64,384]{2,1,0:T(8,128)S(1)}, f32[4,64,384]{2,1,0:T(8,128)S(1)}, u32[]{:S(2)}, u32[]{:S(2)}) collective-permute-start(f32[4,64,384]{2,1,0:T(8,128)S(1)} %collective-permute-done.14.value_ref.freq_ref), channel_id=1, source_target_pairs={{0,2},{2,0},{4,6},{6,4},{8,10},{10,8},{12,14},{14,12},{16,18},{18,... | collective-permute-start | bytes 1179656 | tf_op jit(solution)/shard_map/ppermute | solution.py:324
  72.2 4.6 %copy-start.1 = (bf16[1024,6144]{1,0:T(8,128)(2,1)S(1)}, bf16[1024,6144]{1,0:T(8,128)(2,1)}, u32[]{:S(2)}) copy-start(bf16[1024,6144]{1,0:T(8,128)(2,1)} %geno_ref.31) | copy-start | bytes 37748740
  80.2 18.7 %slice-start = ((s8[12582912]{0:T(1024)(128)(4,1)}), s8[4194304]{0:T(1024)(128)(4,1)S(1)}, s32[]{:S(2)}) async-start(s8[12582912]{0:T(1024)(128)(4,1)} %bitcast.29), calls=%async_computation | async-start | bytes 8388608
  80.2 18.7 %slice-start.1 = ((s8[12582912]{0:T(1024)(128)(4,1)}), s8[4194304]{0:T(1024)(128)(4,1)S(1)}, s32[]{:S(2)}) async-start(s8[12582912]{0:T(1024)(128)(4,1)} %bitcast.29), calls=%async_computation.1 | async-start | bytes 8388608
  82.0 17.0 %slice-start.2 = ((s8[12582912]{0:T(1024)(128)(4,1)}), s8[4194304]{0:T(1024)(128)(4,1)S(1)}, s32[]{:S(2)}) async-start(s8[12582912]{0:T(1024)(128)(4,1)} %bitcast.29), calls=%async_computation.2 | async-start | bytes 8388608
  83.7 14.8 %collective-permute-start.18 = (f32[64,1024]{1,0:T(8,128)S(1)}, f32[64,1024]{1,0:T(8,128)S(1)}, u32[]{:S(2)}, u32[]{:S(2)}) collective-permute-start(f32[64,1024]{1,0:T(8,128)S(1)} %cross_q.11.refs_0_), channel_id=1, source_target_pairs={{0,1},{1,0},{2,3},{3,2},{4,5},{5,4},{6,7},{7,6},{8,9},{9,8},{10,11... | collective-permute-start | bytes 786440 | tf_op jit(solution)/shard_map/ppermute | solution.py:375
  87.0 6.2 %collective-permute-start.17 = (f32[64,64]{1,0:T(8,128)S(1)}, f32[64,64]{1,0:T(8,128)S(1)}, u32[]{:S(2)}, u32[]{:S(2)}) collective-permute-start(f32[64,64]{1,0:T(8,128)S(1)} %gram.14.refs_0_), channel_id=1, source_target_pairs={{0,1},{1,0},{2,3},{3,2},{4,5},{5,4},{6,7},{7,6},{8,9},{9,8},{10,11... | collective-permute-start | bytes 49160 | tf_op jit(solution)/shard_map/ppermute | solution.py:374
  100.2 1.9 %collective-permute-start.25 = (f32[4,64,384]{2,1,0:T(8,128)S(1)}, f32[4,64,384]{2,1,0:T(8,128)S(1)}, u32[]{:S(2)}, u32[]{:S(2)}) collective-permute-start(f32[4,64,384]{2,1,0:T(8,128)S(1)} %cross_p.8), channel_id=1, source_target_pairs={{0,2},{2,0},{4,6},{6,4},{8,10},{10,8},{12,14},{14,12},{16,18},{18,... | collective-permute-start | bytes 1179656 | tf_op jit(solution)/shard_map/ppermute | solution.py:324
  101.5 3.4 %collective-permute-start.24 = (f32[4,64,384]{2,1,0:T(8,128)S(1)}, f32[4,64,384]{2,1,0:T(8,128)S(1)}, u32[]{:S(2)}, u32[]{:S(2)}) collective-permute-start(f32[4,64,384]{2,1,0:T(8,128)S(1)} %cross_p.6), channel_id=1, source_target_pairs={{0,2},{2,0},{4,6},{6,4},{8,10},{10,8},{12,14},{14,12},{16,18},{18,... | collective-permute-start | bytes 1179656 | tf_op jit(solution)/shard_map/ppermute | solution.py:324
  103.3 11.2 %collective-permute-start.26 = (f32[4,64,384]{2,1,0:T(8,128)S(1)}, f32[4,64,384]{2,1,0:T(8,128)S(1)}, u32[]{:S(2)}, u32[]{:S(2)}) collective-permute-start(f32[4,64,384]{2,1,0:T(8,128)S(1)} %cross_p.9), channel_id=1, source_target_pairs={{0,4},{2,6},{4,0},{6,2},{8,12},{10,14},{12,8},{14,10},{16,20},{18,... | collective-permute-start | bytes 1179656 | tf_op jit(solution)/shard_map/ppermute | solution.py:324
  114.5 24.9 %collective-permute-start.27 = (f32[64,384]{1,0:T(8,128)S(1)}, f32[64,384]{1,0:T(8,128)S(1)}, u32[]{:S(2)}, u32[]{:S(2)}) collective-permute-start(f32[64,384]{1,0:T(8,128)S(1)} %get-tuple-element.4), channel_id=1, source_target_pairs={{0,8},{2,10},{4,12},{6,14},{8,16},{10,18},{12,20},{14,22},{16,24},... | collective-permute-start | bytes 294920 | tf_op jit(solution)/shard_map/ppermute | solution.py:324
  116.2 23.2 %collective-permute-start.28 = (f32[64,384]{1,0:T(8,128)S(1)}, f32[64,384]{1,0:T(8,128)S(1)}, u32[]{:S(2)}, u32[]{:S(2)}) collective-permute-start(f32[64,384]{1,0:T(8,128)S(1)} %get-tuple-element.3), channel_id=1, source_target_pairs={{0,16},{2,18},{4,20},{6,22},{8,24},{10,26},{12,28},{14,30},{16,0},... | collective-permute-start | bytes 294920 | tf_op jit(solution)/shard_map/ppermute | solution.py:324
  118.2 21.2 %collective-permute-start.29 = (f32[64,384]{1,0:T(8,128)S(1)}, f32[64,384]{1,0:T(8,128)S(1)}, u32[]{:S(2)}, u32[]{:S(2)}) collective-permute-start(f32[64,384]{1,0:T(8,128)S(1)} %get-tuple-element.2), channel_id=1, source_target_pairs={{0,24},{2,26},{4,28},{6,30},{8,0},{10,2},{12,4},{14,6},{16,8},{18,... | collective-permute-start | bytes 294920 | tf_op jit(solution)/shard_map/ppermute | solution.py:324
  119.1 1.3 collective-permute-start.19
  120.4 3.9 %collective-permute-start.20 = (f32[64,64]{1,0:T(8,128)S(1)}, f32[64,64]{1,0:T(8,128)S(1)}, u32[]{:S(2)}, u32[]{:S(2)}) collective-permute-start(f32[64,64]{1,0:T(8,128)S(1)} %add.125), channel_id=1, source_target_pairs={{0,4},{2,6},{4,0},{6,2},{8,12},{10,14},{12,8},{14,10},{16,20},{18,... | collective-permute-start | bytes 49160 | tf_op jit(solution)/shard_map/ppermute | solution.py:324
  124.3 5.8 %collective-permute-start.21 = (f32[64,64]{1,0:T(8,128)S(1)}, f32[64,64]{1,0:T(8,128)S(1)}, u32[]{:S(2)}, u32[]{:S(2)}) collective-permute-start(f32[64,64]{1,0:T(8,128)S(1)} %add.126.refs_0_), channel_id=1, source_target_pairs={{0,8},{2,10},{4,12},{6,14},{8,16},{10,18},{12,20},{14,22},{16,24},... | collective-permute-start | bytes 49160 | tf_op jit(solution)/shard_map/ppermute | solution.py:324
  125.8 5.2 %collective-permute-start.22 = (f32[64,64]{1,0:T(8,128)S(1)}, f32[64,64]{1,0:T(8,128)S(1)}, u32[]{:S(2)}, u32[]{:S(2)}) collective-permute-start(f32[64,64]{1,0:T(8,128)S(1)} %add.126.refs_0_), channel_id=1, source_target_pairs={{0,16},{2,18},{4,20},{6,22},{8,24},{10,26},{12,28},{14,30},{16,0},... | collective-permute-start | bytes 49160 | tf_op jit(solution)/shard_map/ppermute | solution.py:324
  130.1 3.9 %collective-permute-start.23 = (f32[64,64]{1,0:T(8,128)S(1)}, f32[64,64]{1,0:T(8,128)S(1)}, u32[]{:S(2)}, u32[]{:S(2)}) collective-permute-start(f32[64,64]{1,0:T(8,128)S(1)} %add.126.refs_0_), channel_id=1, source_target_pairs={{0,24},{2,26},{4,28},{6,30},{8,0},{10,2},{12,4},{14,6},{16,8},{18,... | collective-permute-start | bytes 49160 | tf_op jit(solution)/shard_map/ppermute | solution.py:324
  139.7 6.6 %collective-permute-start.32 = (f32[64,384]{1,0:T(8,128)S(1)}, f32[64,384]{1,0:T(8,128)S(1)}, u32[]{:S(2)}, u32[]{:S(2)}) collective-permute-start(f32[64,384]{1,0:T(8,128)S(1)} %apply.6), channel_id=1, source_target_pairs={{0,8},{2,10},{4,12},{6,14},{8,16},{10,18},{12,20},{14,22},{16,24},... | collective-permute-start | bytes 294920 | tf_op jit(solution)/shard_map/ppermute | solution.py:324
  139.7 8.1 %collective-permute-start.31 = (f32[64,384]{1,0:T(8,128)S(1)}, f32[64,384]{1,0:T(8,128)S(1)}, u32[]{:S(2)}, u32[]{:S(2)}) collective-permute-start(f32[64,384]{1,0:T(8,128)S(1)} %apply.6), channel_id=1, source_target_pairs={{0,16},{2,18},{4,20},{6,22},{8,24},{10,26},{12,28},{14,30},{16,0},... | collective-permute-start | bytes 294920 | tf_op jit(solution)/shard_map/ppermute | solution.py:324
  142.1 5.8 %collective-permute-start.30 = (f32[64,384]{1,0:T(8,128)S(1)}, f32[64,384]{1,0:T(8,128)S(1)}, u32[]{:S(2)}, u32[]{:S(2)}) collective-permute-start(f32[64,384]{1,0:T(8,128)S(1)} %apply.6), channel_id=1, source_target_pairs={{0,24},{2,26},{4,28},{6,30},{8,0},{10,2},{12,4},{14,6},{16,8},{18,... | collective-permute-start | bytes 294920 | tf_op jit(solution)/shard_map/ppermute | solution.py:324
  147.9 7.8 %collective-permute-start.33 = (f32[4,64,384]{2,1,0:T(8,128)S(1)}, f32[4,64,384]{2,1,0:T(8,128)S(1)}, u32[]{:S(2)}, u32[]{:S(2)}) collective-permute-start(f32[4,64,384]{2,1,0:T(8,128)S(1)} %pad_maximum_fusion.1.value_ref.freq_ref.refs_0_), channel_id=1, source_target_pairs={{0,4},{2,6},{4,0},{6,2},{8,12},{10,14},{12,8},{14,10},{16,20},{18,... | collective-permute-start | bytes 1179656 | tf_op jit(solution)/shard_map/ppermute | solution.py:324
  149.5 8.0 %collective-permute-start.35 = (f32[4,64,384]{2,1,0:T(8,128)S(1)}, f32[4,64,384]{2,1,0:T(8,128)S(1)}, u32[]{:S(2)}, u32[]{:S(2)}) collective-permute-start(f32[4,64,384]{2,1,0:T(8,128)S(1)} %pad_maximum_fusion.1.value_ref.freq_ref.refs_0_), channel_id=1, source_target_pairs={{0,2},{2,0},{4,6},{6,4},{8,10},{10,8},{12,14},{14,12},{16,18},{18,... | collective-permute-start | bytes 1179656 | tf_op jit(solution)/shard_map/ppermute | solution.py:324
  155.7 5.2 %collective-permute-start.34 = (f32[4,64,384]{2,1,0:T(8,128)S(1)}, f32[4,64,384]{2,1,0:T(8,128)S(1)}, u32[]{:S(2)}, u32[]{:S(2)}) collective-permute-start(f32[4,64,384]{2,1,0:T(8,128)S(1)} %collective-permute-done.33.value_ref.freq_ref.refs_2_), channel_id=1, source_target_pairs={{0,2},{2,0},{4,6},{6,4},{8,10},{10,8},{12,14},{14,12},{16,18},{18,... | collective-permute-start | bytes 1179656 | tf_op jit(solution)/shard_map/ppermute | solution.py:324
  162.7 14.9 %collective-permute-start.37 = (f32[64,1024]{1,0:T(8,128)S(1)}, f32[64,1024]{1,0:T(8,128)S(1)}, u32[]{:S(2)}, u32[]{:S(2)}) collective-permute-start(f32[64,1024]{1,0:T(8,128)S(1)} %cross_q.15.refs_0_), channel_id=1, source_target_pairs={{0,1},{1,0},{2,3},{3,2},{4,5},{5,4},{6,7},{7,6},{8,9},{9,8},{10,11... | collective-permute-start | bytes 786440 | tf_op jit(solution)/shard_map/ppermute | solution.py:375
  165.9 6.2 %collective-permute-start.36 = (f32[64,64]{1,0:T(8,128)S(1)}, f32[64,64]{1,0:T(8,128)S(1)}, u32[]{:S(2)}, u32[]{:S(2)}) collective-permute-start(f32[64,64]{1,0:T(8,128)S(1)} %gram.19.refs_0_), channel_id=1, source_target_pairs={{0,1},{1,0},{2,3},{3,2},{4,5},{5,4},{6,7},{7,6},{8,9},{9,8},{10,11... | collective-permute-start | bytes 49160 | tf_op jit(solution)/shard_map/ppermute | solution.py:374
